TPU v7x, 32 devices: a whole 2x2x4 slice. The times are simulated.
32 devices in a mesh: seg: 4 (over y, core), ep: 8 (over z, x).
Axes of the slice: x: 2, y: 2, z: 4, core: 2. Of those that a mesh axis runs over, the one named last changes fastest.
Arguments:
- queries: bfloat16 [2048, 2048], P(('seg', 'ep')), may hold values from -6 to 6
- keys: bfloat16 [2048, 2048], P(('seg', 'ep')), may hold values from -1.25 to 1.25
- values: bfloat16 [2048, 2048], P(('seg', 'ep')), may hold values from -54 to 54
- log_decay: float32 [2048, 16], P('seg', 'ep'), may hold values from -1 to 0
- out_gain: float32 [2048], replicated, may hold values from 0.1 to 1.9
- out_proj: bfloat16 [2048, 6144], P('ep', 'seg'), may hold values from -0.125 to 0.125
- experts: int32 [256, 2], P(('seg', 'ep')), may hold values from 0 to 3, all different within a row; in each aligned block of 8 rows (0 to 7, 8 to 15, ...) at most 8 rows name the same one
- gates: float32 [256, 2], P(('seg', 'ep')), may hold values from 0.2 to 1
- up_weight: bfloat16 [8, 6144, 2304], P('ep', None, 'seg'), may hold values from -0.078125 to 0.078125
- down_weight: bfloat16 [8, 2304, 6144], P('ep', 'seg'), may hold values from -0.09375 to 0.09375
Outputs:
- attn_out: bfloat16 [2048, 2048], P(('seg', 'ep'))
- moe_out: bfloat16 [256, 6144], P(('seg', 'ep'))
Inputs may be any that keep to these rules, and one draw needn't show every extreme that they name: Each row names two different experts. The 8 rows of one device name any one expert at most 8 times, and in some devices one expert exactly 8 times.
All inputs are finite; a program needn't handle non-finite values.
Results may differ from a plain program's by a relative error of at most 0.025.
Values may be sent and summed in bfloat16 or wider, within the bound.
A program may use at most 128 MiB of HBM per device.

v0:
```python
import functools
import math

import jax
import jax.numpy as jnp
from jax import lax
from jax.experimental import pallas as pl
from jax.experimental.pallas import tpu as pltpu
from jax.sharding import PartitionSpec as P

epsilon = 1e-06
MESH = pl.DeviceIdType.MESH
VM = pltpu.VMEM


def prefix(x, axis, join, neutral):
    place = lax.axis_index(axis)
    gathered = jax.tree.map(
        lambda a, kind: lax.all_gather(a.astype(kind), axis), x, (jnp.bfloat16, jnp.bfloat16)
    )
    state = jax.tree.map(lambda a, e: jnp.zeros_like(a) + jnp.asarray(e, a.dtype), x, neutral)

    def one(turn, state):
        return join(
            state,
            jax.tree.map(
                lambda a, own: lax.dynamic_index_in_dim(a, turn, 0, False).astype(own.dtype),
                gathered,
                x,
            ),
        )

    return lax.fori_loop(0, place, one, state)


def chain_combine(first_part, second_part):
    return (
        first_part[0] * second_part[0],
        second_part[0][:, None, None] * first_part[1] + second_part[1],
    )


def route_tables(experts, gates, expert_count, capacity):
    token_count = experts.shape[0]
    flattened = experts.reshape(-1)
    onehot = (flattened[:, None] == jnp.arange(expert_count, dtype=jnp.int32)[None, :]).astype(
        jnp.int32
    )
    earlier = jnp.cumsum(onehot, axis=0) - onehot
    position = jnp.sum(earlier * onehot, axis=1)
    slot_index = (flattened * capacity + position).reshape(token_count, 2)
    columns = jnp.arange(expert_count * capacity, dtype=jnp.int32)
    matches = slot_index[:, :, None] == columns[None, None, :]
    dispatch = jnp.any(matches, axis=1).T.astype(jnp.bfloat16)
    combine = jnp.sum(jnp.where(matches, gates[:, :, None], 0.0), axis=1)
    return (dispatch, combine)


def expert_output(row_data, up_piece, down_piece):
    hidden = jax.nn.silu(jnp.dot(row_data, up_piece, preferred_element_type=jnp.float32)).astype(
        jnp.bfloat16
    )
    return jnp.dot(hidden, down_piece, preferred_element_type=jnp.float32)


def on_device_routed(
    queries, keys, values, log_decay, out_gain, out_proj, experts, gates, up_weight, down_weight
):
    highest = lax.Precision.HIGHEST
    ep_count = lax.axis_size("ep")
    heads_local = log_decay.shape[1]
    head_dim = queries.shape[1] // (heads_local * ep_count)
    query_heads, key_heads, value_heads = (
        lax.all_to_all(queries, "ep", split_axis=1, concat_axis=0, tiled=True),
        lax.all_to_all(keys, "ep", split_axis=1, concat_axis=0, tiled=True),
        lax.all_to_all(values, "ep", split_axis=1, concat_axis=0, tiled=True),
    )
    seg_length = query_heads.shape[0]
    query_heads = query_heads.reshape(seg_length, heads_local, head_dim)
    key_heads = key_heads.reshape(seg_length, heads_local, head_dim)
    value_heads = value_heads.reshape(seg_length, heads_local, head_dim)
    cumulative = jnp.cumsum(log_decay, axis=0)
    across = cumulative.T
    block_size = math.gcd(seg_length, 512)
    starts = jnp.arange(seg_length // block_size, dtype=jnp.int32) * block_size
    token_positions = jnp.arange(seg_length, dtype=jnp.int32)

    def block_mix(start):
        query_block = lax.dynamic_slice_in_dim(query_heads, start, block_size, 0)
        cum_block = lax.dynamic_slice_in_dim(across, start, block_size, 1)
        row_ids = start + jnp.arange(block_size, dtype=jnp.int32)
        causal = (row_ids[:, None] >= token_positions[None, :])[None]
        log_gap = cum_block[:, :, None] - across[:, None, :]
        weight = jnp.where(causal, jnp.exp(jnp.where(causal, log_gap, 0.0)), 0.0)
        scores = jnp.einsum(
            "thd,shd->hts", query_block, key_heads, preferred_element_type=jnp.float32
        )
        mixing = (scores * weight).astype(jnp.bfloat16)
        return jnp.einsum("hts,she->the", mixing, value_heads, preferred_element_type=jnp.float32)

    inside = lax.map(block_mix, starts).reshape(seg_length, heads_local, head_dim)
    ending = cumulative[-1]
    to_end = jnp.exp(ending[None, :] - cumulative)
    key_float = key_heads.astype(jnp.float32)
    value_float = value_heads.astype(jnp.float32)
    local_state = jnp.einsum("sh,shd,she->hde", to_end, key_float, value_float, precision=highest)
    identity = (jnp.ones_like(ending), jnp.zeros_like(local_state))
    carried = prefix((jnp.exp(ending), local_state), "seg", chain_combine, identity)[1]
    outside = jnp.exp(cumulative)[:, :, None] * jnp.einsum(
        "thd,hde->the", query_heads.astype(jnp.float32), carried, precision=highest
    )
    mixture = (inside + outside).astype(jnp.bfloat16).reshape(seg_length, heads_local * head_dim)
    token_mix = lax.all_to_all(mixture, "ep", split_axis=0, concat_axis=1, tiled=True)
    as_float = token_mix.astype(jnp.float32)
    inv_rms = lax.rsqrt(jnp.mean(as_float * as_float, axis=1, keepdims=True) + epsilon)
    attn_out = (as_float * inv_rms * out_gain[None, :]).astype(jnp.bfloat16)
    row_stride = 8
    own_width = heads_local * head_dim
    feature_count = own_width * ep_count
    picked_float = mixture.reshape(seg_length // row_stride, row_stride, own_width)[:, 0].astype(
        jnp.float32
    )
    square_sums = lax.psum(jnp.sum(picked_float * picked_float, axis=1), "ep")
    picked_rms = lax.rsqrt(square_sums[:, None] / feature_count + epsilon)
    gain_slice = lax.dynamic_slice_in_dim(out_gain, lax.axis_index("ep") * own_width, own_width, 0)
    normed_rows = (picked_float * picked_rms * gain_slice[None, :]).astype(jnp.bfloat16)
    proj_terms = jnp.dot(
        normed_rows,
        lax.all_gather(out_proj, "seg", axis=1, tiled=True),
        preferred_element_type=jnp.float32,
    )
    moe_in = lax.psum_scatter(
        proj_terms.astype(jnp.bfloat16), "ep", scatter_dimension=0, tiled=True
    )
    expert_count = ep_count // 2
    token_count, model_width = moe_in.shape
    capacity = max(2, 4 * token_count // expert_count)
    dispatch, combine = route_tables(experts, gates, expert_count, capacity)
    up_piece = up_weight[0]
    down_piece = down_weight[0]
    slot_rows = jnp.dot(dispatch, moe_in, preferred_element_type=jnp.float32).astype(jnp.bfloat16)
    outgoing = jnp.repeat(slot_rows.reshape(expert_count, capacity, model_width), 2, axis=0)
    arrived = lax.all_to_all(outgoing, "ep", split_axis=0, concat_axis=0, tiled=True).reshape(
        ep_count * capacity, model_width
    )
    gathered = lax.all_gather(arrived, "seg", axis=0, tiled=True)
    owned_sums = lax.psum_scatter(
        expert_output(gathered, up_piece, down_piece).astype(jnp.bfloat16),
        "seg",
        scatter_dimension=0,
        tiled=True,
    ).astype(jnp.float32)
    returned_back = lax.all_to_all(
        owned_sums.reshape(ep_count, capacity, model_width).astype(jnp.bfloat16),
        "ep",
        split_axis=0,
        concat_axis=0,
        tiled=True,
    ).astype(jnp.float32)
    paired = returned_back.reshape(expert_count, 2, capacity, model_width)
    halves = (paired[:, 0] + paired[:, 1]).reshape(expert_count * capacity, model_width)
    summed = jnp.dot(combine, halves, precision=highest)
    moe_out = summed.astype(jnp.bfloat16)
    return (attn_out, moe_out)


def remote(src, dst, send, recv, **target):
    return pltpu.make_async_remote_copy(
        src_ref=src, dst_ref=dst, send_sem=send, recv_sem=recv,
        device_id=target, device_id_type=MESH,
    )


def greet(seg_count, ep_count):
    seg, ep = lax.axis_index("seg"), lax.axis_index("ep")
    barrier = pltpu.get_barrier_semaphore()
    for j in range(1, ep_count):
        pl.semaphore_signal(
            barrier, inc=1, device_id={"ep": lax.rem(ep + j, ep_count)}, device_id_type=MESH
        )
    for k in range(1, seg_count):
        pl.semaphore_signal(
            barrier, inc=1, device_id={"seg": lax.rem(seg + k, seg_count)}, device_id_type=MESH
        )
    pl.semaphore_wait(barrier, ep_count + seg_count - 2)
    return seg, ep


def step_kernel(
    seg_count, ep_count, heads, dim, tile,
    q_ref, k_ref, v_ref, proj_hbm, up_hbm, down_hbm,
    decay_ref, turned_ref, experts_ref, gates_ref, gain_ref,
    attn_ref, out_ref,
    qb, kb, vb, states, ends, table_ref, mix_ref,
    up, down, proj, rows, part, sums, full, acc, hidden, tokens,
    terms, core_in, both, y_in, x_in, middle, line, line_in,
    load_sem, in_send, in_recv, gate_send, gate_recv,
    st_send, st_recv, end_send, end_recv, row_send, row_recv, pick_send, pick_recv,
    rs_send, rs_recv, ag_send, ag_recv, x_send, x_recv, y_send, y_recv, c_send, c_recv,
    t_send, t_recv, tc_send, tc_recv, ty_send, ty_recv, tx_send, tx_recv, tz_send, tz_recv,
):
    seg, ep = greet(seg_count, ep_count)
    width = heads * dim
    tokens_own, moe_own = q_ref.shape[0], experts_ref.shape[0]
    triples = ((k_ref, kb), (v_ref, vb), (q_ref, qb))
    sends = {}
    own = pl.ds(pl.multiple_of(ep * width, width), width)
    keep = []
    for i, (ref, buf) in enumerate(triples):
        sends[i] = []
        for j in range(1, ep_count):
            other = lax.rem(ep + j, ep_count)
            columns = pl.ds(pl.multiple_of(other * width, width), width)
            copy = remote(
                ref.at[:, columns], buf.at[ep], in_send.at[i, j], in_recv.at[i, j], ep=other
            )
            copy.start()
            sends[i].append(copy)
        copy = pltpu.make_async_copy(ref.at[:, own], buf.at[ep], load_sem.at[3 + i])
        copy.start()
        keep.append(copy)
    loads = [
        pltpu.make_async_copy(proj_hbm, proj, load_sem.at[0]),
        pltpu.make_async_copy(up_hbm.at[0], up, load_sem.at[1]),
        pltpu.make_async_copy(down_hbm.at[0], down, load_sem.at[2]),
    ]
    for load in loads:
        load.start()
    lanes = lax.broadcasted_iota(jnp.int32, (moe_own, 128), 1)
    table_ref[seg, ep] = sum(
        jnp.where(experts_ref[:, i : i + 1] == lanes, gates_ref[:, i : i + 1], 0.0)
        for i in range(experts_ref.shape[1])
    )
    gates = []
    for j in range(1, ep_count):
        copy = remote(
            table_ref.at[seg, ep], table_ref.at[seg, ep], gate_send.at[j], gate_recv.at[j],
            ep=lax.rem(ep + j, ep_count),
        )
        copy.start()
        gates.append(copy)
    length = tokens_own * ep_count
    highest = lax.Precision.HIGHEST
    rows_at = lax.broadcasted_iota(jnp.int32, (length, length), 0)
    columns_at = lax.broadcasted_iota(jnp.int32, (length, length), 1)
    causal = rows_at >= columns_at
    lower = causal.astype(jnp.float32)
    cum = jnp.dot(lower, decay_ref[...], precision=highest, preferred_element_type=jnp.float32)
    across = lax.dot_general(
        turned_ref[...], lower, (((1,), (1,)), ((), ())), precision=highest,
        preferred_element_type=jnp.float32,
    )
    for copy in keep:
        copy.wait()
    for i in (0, 1):
        for copy in sends[i]:
            copy.wait()
    keys, values = (
        jnp.concatenate([b[p] for p in range(ep_count)], axis=0) for b in (kb, vb)
    )
    ending = cum[length - 1 : length, :]
    unit = (
        lax.broadcasted_iota(jnp.int32, (dim, dim), 0)
        == lax.broadcasted_iota(jnp.int32, (dim, dim), 1)
    ).astype(jnp.float32).astype(jnp.bfloat16)
    for h in range(heads):
        cols = slice(h * dim, (h + 1) * dim)
        to_end = jnp.exp(ending[:, h : h + 1] - across[h : h + 1, :])
        turned = lax.dot_general(
            unit, keys[:, cols], (((1,), (1,)), ((), ())), preferred_element_type=jnp.float32
        )
        states[seg, h] = jnp.dot(
            (turned * to_end).astype(jnp.bfloat16), values[:, cols],
            preferred_element_type=jnp.float32,
        ).astype(jnp.bfloat16)
        ends[seg, h : h + 1] = jnp.broadcast_to(ending[:, h : h + 1], (1, dim))
    for copy in gates:
        copy.wait()
    moved = []
    for k in range(1, seg_count):
        other = lax.rem(seg + k, seg_count)
        for buf, send, recv in (
            (states, st_send, st_recv), (ends, end_send, end_recv), (table_ref, row_send, row_recv)
        ):
            copy = remote(buf.at[seg], buf.at[seg], send.at[k], recv.at[k], seg=other)
            copy.start()
            moved.append(copy)
    for copy in sends[2]:
        copy.wait()
    queries = jnp.concatenate([qb[p] for p in range(ep_count)], axis=0)
    inside = []
    for h in range(heads):
        cols = slice(h * dim, (h + 1) * dim)
        gap = cum[:, h : h + 1] - across[h : h + 1, :]
        weight = jnp.where(causal, jnp.exp(jnp.where(causal, gap, 0.0)), 0.0)
        scores = lax.dot_general(
            queries[:, cols], keys[:, cols], (((1,), (1,)), ((), ())),
            preferred_element_type=jnp.float32,
        )
        inside.append(
            jnp.dot(
                (scores * weight).astype(jnp.bfloat16), values[:, cols],
                preferred_element_type=jnp.float32,
            )
        )
    for copy in moved:
        copy.wait()
    outs = []
    for h in range(heads):
        cols = slice(h * dim, (h + 1) * dim)
        carried = jnp.zeros((dim, dim), jnp.float32)
        for c in range(seg_count):
            joined = jnp.exp(ends[c, h : h + 1]) * carried + states[c, h].astype(jnp.float32)
            carried = jnp.where(c < seg, joined, carried)
        outside = jnp.exp(cum[:, h : h + 1]) * jnp.dot(
            queries[:, cols], carried.astype(jnp.bfloat16), preferred_element_type=jnp.float32
        )
        outs.append((inside[h] + outside).astype(jnp.bfloat16))
    mixture = jnp.concatenate(outs, axis=1)
    mix_ref[...] = mixture.reshape(mix_ref.shape)
    count = length // tokens_own * moe_own
    stride = length // count
    pick = (
        lax.broadcasted_iota(jnp.int32, (count, length), 1)
        == stride * lax.broadcasted_iota(jnp.int32, (count, length), 0)
    )
    rows[seg] = jnp.dot(
        pick.astype(jnp.float32).astype(jnp.bfloat16), mixture, preferred_element_type=jnp.float32
    ).astype(jnp.bfloat16)
    f32, bf16 = jnp.float32, jnp.bfloat16
    y_count = seg_count // 2
    core, y = lax.rem(seg, 2), lax.div(seg, 2)
    mate = seg + 1 - 2 * core
    own_rows = rows.shape[1]
    total = own_rows * seg_count
    chunk = total // ep_count
    cols = proj.shape[1]
    moved = []
    for k in range(1, seg_count):
        copy = remote(
            rows.at[seg], rows.at[seg], pick_send.at[k], pick_recv.at[k],
            seg=lax.rem(seg + k, seg_count),
        )
        copy.start()
        moved.append(copy)
    for copy in moved:
        copy.wait()
    picked = rows[...].reshape(total, width).astype(f32)
    squares = jnp.sum(picked * picked, axis=1, keepdims=True)
    high = squares.astype(bf16).astype(f32)
    lane = lax.broadcasted_iota(jnp.int32, (total, 128), 1)
    pair = jnp.where(lane < 64, high, squares - high).astype(bf16)
    part[:, :, cols:] = pair.reshape(ep_count, chunk, 128)
    scaled = (picked * gain_ref[:, own]).astype(bf16)
    loads[0].wait()
    for n in range(0, cols, tile):
        part[:, :, n : n + tile] = (
            jnp.dot(scaled, proj[:, n : n + tile], preferred_element_type=f32)
            .astype(bf16)
            .reshape(ep_count, chunk, tile)
        )
    moved = []
    for j in range(1, ep_count):
        other = lax.rem(ep + j, ep_count)
        copy = remote(part.at[other], sums.at[j], rs_send.at[j], rs_recv.at[j], ep=other)
        copy.start()
        moved.append(copy)
    summed = part[ep].astype(f32)
    for j, copy in enumerate(moved):
        copy.wait()
        summed = summed + sums[j + 1].astype(f32)
    features = width * ep_count
    square = summed[:, cols : cols + 1] + summed[:, cols + 64 : cols + 65]
    inv_rms = lax.rsqrt(square / features + epsilon)
    full[seg, ep] = (summed[:, :cols] * inv_rms).astype(bf16)
    half = ep_count // 2
    x, z = lax.rem(ep, 2), lax.div(ep, 2)
    x_mate = ep + 1 - 2 * x
    flying = []

    def send(place, send_sem, recv_sem, **target):
        copy = remote(place, place, send_sem, recv_sem, **target)
        copy.start()
        flying.append(copy)
        return copy

    def on_line(e, k):
        return lax.rem(e - 2 * k + ep_count, ep_count)

    def y_seg(k):
        return lax.rem(y + k + y_count, y_count) * 2 + core

    z_copies = {}
    for k in range(1, half):
        z_copies[k] = send(
            full.at[seg, ep], ag_send.at[k], ag_recv.at[k], ep=lax.rem(ep + 2 * k, ep_count)
        )
    x_copies, y_copies = {}, {}
    for k in range(half):
        if k > 0:
            z_copies[k].wait_recv()
        place = full.at[seg, on_line(ep, k)]
        x_copies[k, 0] = send(place, x_send.at[k, 0], x_recv.at[k, 0], ep=x_mate)
        for d in range(1, y_count):
            y_copies[k, 0, d] = send(
                place, y_send.at[k, 0, d], y_recv.at[k, 0, d], seg=y_seg(d)
            )
        send(place, c_send.at[k, 0, 0], c_recv.at[k, 0, 0], seg=mate)
    for k in range(half):
        x_copies[k, 0].wait_recv()
        place = full.at[seg, on_line(x_mate, k)]
        if k % 2 == 0:
            for d in range(1, y_count):
                y_copies[k, 1, d] = send(
                    place, y_send.at[k, 1, d], y_recv.at[k, 1, d], seg=y_seg(d)
                )
        send(place, c_send.at[k, 1, 0], c_recv.at[k, 1, 0], seg=mate)
        for d in range(1, y_count):
            y_copies[k, 0, d].wait_recv()
            place = full.at[y_seg(-d), on_line(ep, k)]
            if k % 2 == 1:
                x_copies[k, d] = send(place, x_send.at[k, d], x_recv.at[k, d], ep=x_mate)
            send(place, c_send.at[k, 0, d], c_recv.at[k, 0, d], seg=mate)
    loads[1].wait()
    acc[...] = jnp.zeros_like(acc)

    def multiply(s):
        def step(n, carry):
            at = pl.multiple_of(n * tile, tile)
            block = full[s, :, :, pl.ds(at, tile)].reshape(total, tile)
            lines = pl.ds(pl.multiple_of(s * cols + n * tile, tile), tile)
            acc[...] += lax.dot_general(
                block, up[:, lines], (((1,), (1,)), ((), ())), preferred_element_type=f32
            )
            return carry

        lax.fori_loop(0, cols // tile, step, 0)

    multiply(seg)
    for k in range(half):
        for d in range(1, y_count):
            (y_copies[k, 1, d] if k % 2 == 0 else x_copies[k, d]).wait_recv()
            send(
                full.at[y_seg(-d), on_line(x_mate, k)],
                c_send.at[k, 1, d], c_recv.at[k, 1, d], seg=mate,
            )
    for d in range(1, y_count):
        multiply(y_seg(-d))
    for k in range(half):
        for i in range(2):
            for d in range(y_count):
                place = full.at[seg, ep]
                remote(place, place, c_send.at[k, i, d], c_recv.at[k, i, d], seg=mate).wait_recv()
    for copy in flying:
        copy.wait_send()
    backs = []
    tokens[ep] = mix_ref[ep]
    for j in range(1, ep_count):
        other = lax.rem(ep + j, ep_count)
        copy = remote(mix_ref.at[other], tokens.at[ep], t_send.at[j], t_recv.at[j], ep=other)
        copy.start()
        backs.append(copy)
    for k in range(y_count):
        multiply(lax.rem(y + k, y_count) * 2 + 1 - core)
    value = acc[...]
    hidden[...] = (value / (1.0 + jnp.exp(-value))).astype(bf16)
    table = table_ref[...].reshape(total, 128)
    gate = jnp.sum(jnp.where(lane == lax.div(ep, 2), table, 0.0), axis=1, keepdims=True)
    loads[2].wait()
    steps = seg_count
    core_moves = {}

    def product(c):
        for n in range(0, cols, tile):
            at = c * cols + n
            value = jnp.dot(hidden[...], down[:, at : at + tile], preferred_element_type=f32)
            value = jnp.where(gate != 0.0, value * gate, 0.0).astype(bf16)
            terms[c, :, :, n : n + tile] = value.reshape(seg_count, own_rows, tile)
        core_moves[c] = []
        for k in range(y_count):
            copy = remote(
                terms.at[c, k * 2 + 1 - core], core_in.at[c, k],
                tc_send.at[c, k], tc_recv.at[c, k], seg=mate,
            )
            copy.start()
            core_moves[c].append(copy)

    first, second, last = {}, {}, {}
    mine = own_rows // ep_count

    def joined(c):
        for copy in core_moves[c]:
            copy.wait()
        for k in range(y_count):
            value = (terms[c, k * 2 + core].astype(f32) + core_in[c, k].astype(f32)).reshape(
                half, 2, mine, cols
            ).astype(bf16)
            for i in range(2):
                both[c, k, i] = value[:, i]
        first[c] = []
        if c % 2 == 0:
            for d in range(1, y_count):
                first[c].append(
                    remote(
                        both.at[c, lax.rem(y + d, y_count)], y_in.at[c, d],
                        ty_send.at[c, d], ty_recv.at[c, d], seg=y_seg(d),
                    )
                )
        else:
            first[c].append(
                remote(
                    both.at[c, :, 1 - x], x_in.at[c], tx_send.at[c], tx_recv.at[c], ep=x_mate
                )
            )
        for copy in first[c]:
            copy.start()

    def crossed(c):
        for copy in first[c]:
            copy.wait()
        second[c] = []
        if c % 2 == 0:
            for i in range(2):
                value = both[c, y, i].astype(f32)
                for d in range(1, y_count):
                    value = value + y_in[c, d, i].astype(f32)
                middle[c, i] = value.astype(bf16)
            second[c].append(
                remote(
                    middle.at[c, 1 - x], x_in.at[c, 0], tx_send.at[c], tx_recv.at[c], ep=x_mate
                )
            )
        else:
            for k in range(y_count):
                middle[c, k] = (both[c, k, x].astype(f32) + x_in[c, k].astype(f32)).astype(bf16)
            for d in range(1, y_count):
                second[c].append(
                    remote(
                        middle.at[c, lax.rem(y + d, y_count)], y_in.at[c, d, 0],
                        ty_send.at[c, d], ty_recv.at[c, d], seg=y_seg(d),
                    )
                )
        for copy in second[c]:
            copy.start()

    def along(c):
        for copy in second[c]:
            copy.wait()
        if c % 2 == 0:
            value = middle[c, x].astype(f32) + x_in[c, 0].astype(f32)
        else:
            value = middle[c, y].astype(f32)
            for d in range(1, y_count):
                value = value + y_in[c, d, 0].astype(f32)
        line[c] = value.astype(bf16)
        last[c] = []
        for k in range(1, half):
            other = lax.rem(z + k, half)
            copy = remote(
                line.at[c, other], line_in.at[c, k], tz_send.at[c, k], tz_recv.at[c, k],
                ep=other * 2 + x,
            )
            copy.start()
            last[c].append(copy)

    for c in range(steps + 3):
        if c < steps:
            product(c)
        if 0 <= c - 1 < steps:
            joined(c - 1)
        if 0 <= c - 2 < steps:
            crossed(c - 2)
        if 0 <= c - 3 < steps:
            along(c - 3)
    for copy in backs:
        copy.wait()
    mixed = [tokens[p].astype(f32) for p in range(ep_count)]
    square = sum(jnp.sum(m * m, axis=1, keepdims=True) for m in mixed)
    inv_rms = lax.rsqrt(square / features + epsilon)
    for p in range(ep_count):
        at = slice(p * width, (p + 1) * width)
        attn_ref[:, at] = (mixed[p] * inv_rms * gain_ref[:, at]).astype(bf16)
    for c in range(steps):
        value = line[c, z].astype(f32)
        for j, copy in enumerate(last[c]):
            copy.wait()
            value = value + line_in[c, j + 1].astype(f32)
        out_ref[:, c * cols : (c + 1) * cols] = value.astype(bf16)


def on_device_dense(
    queries, keys, values, log_decay, out_gain, out_proj, experts, gates, up_weight, down_weight
):
    f32, bf16 = jnp.float32, jnp.bfloat16
    dma = pltpu.SemaphoreType.DMA
    seg_count, ep_count = lax.axis_size("seg"), lax.axis_size("ep")
    y_count, half = seg_count // 2, ep_count // 2
    tokens_own, features = queries.shape
    heads = log_decay.shape[1]
    width = features // ep_count
    dim = width // heads
    moe_own = experts.shape[0]
    seg_rows = moe_own * ep_count
    total = seg_rows * seg_count
    cols = out_proj.shape[1]
    model, units = up_weight.shape[1:]
    chunk = total // ep_count
    vmem = pl.BlockSpec(memory_space=pltpu.VMEM)
    hbm = pl.BlockSpec(memory_space=pl.ANY)
    return pl.pallas_call(
        functools.partial(step_kernel, seg_count, ep_count, heads, dim, math.gcd(cols, 512)),
        out_shape=(
            jax.ShapeDtypeStruct((tokens_own, features), bf16),
            jax.ShapeDtypeStruct((moe_own, model), bf16),
        ),
        in_specs=[hbm] * 6 + [vmem] * 5,
        out_specs=(vmem, vmem),
        scratch_shapes=[VM((ep_count, tokens_own, width), bf16)] * 3
        + [
            VM((seg_count, heads, dim, dim), bf16),
            VM((seg_count, 8, dim), f32),
            VM((seg_count, ep_count, moe_own, 128), f32),
            VM((ep_count, tokens_own, width), bf16),
            VM((units, model), bf16),
            VM((units, model), bf16),
            VM((width, cols), bf16),
            VM((seg_count, seg_rows, width), bf16),
            VM((ep_count, chunk, cols + 128), bf16),
            VM((ep_count, chunk, cols + 128), bf16),
            VM((seg_count, ep_count, chunk, cols), bf16),
            VM((total, units), f32),
            VM((total, units), bf16),
            VM((ep_count, tokens_own, width), bf16),
            VM((seg_count, seg_count, seg_rows, cols), bf16),
            VM((seg_count, y_count, seg_rows, cols), bf16),
            VM((seg_count, y_count, 2, half, moe_own, cols), bf16),
            VM((seg_count, y_count, 2, half, moe_own, cols), bf16),
            VM((seg_count, y_count, half, moe_own, cols), bf16),
            VM((seg_count, max(2, y_count), half, moe_own, cols), bf16),
            VM((seg_count, half, moe_own, cols), bf16),
            VM((seg_count, half, moe_own, cols), bf16),
            dma((6,)),
        ]
        + [dma((3, ep_count))] * 2
        + [dma((ep_count,))] * 2
        + [dma((seg_count,))] * 8
        + [dma((ep_count,))] * 2
        + [dma((half,))] * 2
        + [dma((half, y_count))] * 2
        + [dma((half, 2, y_count))] * 4
        + [dma((ep_count,))] * 2
        + [dma((seg_count, y_count))] * 4
        + [dma((seg_count,))] * 2
        + [dma((seg_count, half))] * 2,
        compiler_params=pltpu.CompilerParams(
            collective_id=1, has_side_effects=True, vmem_limit_bytes=62 * 2**20
        ),
    )(
        queries, keys, values, out_proj, jnp.swapaxes(up_weight, 1, 2), down_weight,
        log_decay, log_decay.T, experts, gates, out_gain[None, :],
    )


def on_device(*args):
    experts, ep_count = args[6], lax.axis_size("ep")
    full_rows = max(2, 4 * experts.shape[0] // (ep_count // 2)) >= experts.shape[0]
    return (on_device_dense if full_rows else on_device_routed)(*args)


def solution(mesh):
    placed = (
        P(("seg", "ep"), None),
        P(("seg", "ep"), None),
        P(("seg", "ep"), None),
        P("seg", "ep"),
        P(),
        P("ep", "seg"),
        P(("seg", "ep"), None),
        P(("seg", "ep"), None),
        P("ep", None, "seg"),
        P("ep", "seg", None),
    )
    return jax.shard_map(
        on_device,
        mesh=mesh,
        in_specs=placed,
        out_specs=(P(("seg", "ep"), None), P(("seg", "ep"), None)),
        check_vma=False,
    )
```

profile of v0, /device:TPU:0, one launch (start us, length us, event | category | flops | bytes accessed | tf_op | source)
XLA Modules:
  0.0 118.9 jit_solution(17902622090524277791)
XLA Ops:
  0.6 1.3 %copy.13.experts_ref = s32[8,2]{1,0:T(8,128)} copy(s32[8,2]{0,1:T(2,128)} %param.16) | data formatting | bytes 128 | tf_op args[6]
  2.0 1.3 %copy.14.gates_ref = f32[8,2]{1,0:T(8,128)} copy(f32[8,2]{0,1:T(2,128)} %param.17) | data formatting | bytes 128 | tf_op args[7]
  3.3 1.5 %copy.12.decay_ref = f32[512,2]{1,0:T(8,128)} copy(f32[512,2]{0,1:T(2,128)} %param.13) | data formatting | bytes 8192 | tf_op args[3]
  4.9 110.8 %shard_map.113 = (bf16[64,2048]{1,0:T(8,128)(2,1)}, bf16[8,6144]{1,0:T(8,128)(2,1)}) custom-call(bf16[64,2048]{1,0:T(8,128)(2,1)} %q_ref.1, bf16[64,2048]{1,0:T(8,128)(2,1)} %k_ref.1, bf16[64,2048]{1,0:T(8,128)(2,1)} %v_ref.1, bf16[256,1536]{1,0:T(8,128)(2,1)} %proj_hbm.1, bf16[1,576,6144]{2,1,0:T(8,128)(2,1)} %bitcast.3, bf16[1,576,6144]{2,1,0:T(8,128)(2,1)} %down_hbm.1, ...), custom_call_target="tpu_custom_call" | custom-call | tf_op jit(solution)/shard_map/pallas_call | solution.py:610
  115.6 1.7 %copy.17 = bf16[64,2048]{1,0:T(8,128)(2,1)} copy(bf16[64,2048]{1,0:T(8,128)(2,1)} %get-tuple-element.4) | data formatting | bytes 524288
  117.3 1.5 %copy.18 = bf16[8,6144]{1,0:T(8,128)(2,1)} copy(bf16[8,6144]{1,0:T(8,128)(2,1)} %get-tuple-element.5) | data formatting | bytes 196608
where the time goes:
time: 119 us
  Pallas kernels  111 us (93%)
  local copies, waits for them, and re-layouts  7.44 us (6%)
    pallas_call x1, Pallas kernels, on_device_dense(): pl.pallas_call(functools.partial(step_kernel, seg_count, ep_count, heads,...  111 us
    unnamed x5, local copies, waits for them, and re-layouts  7.44 us

commit v1 on v0

--- a/solution.py
+++ b/solution.py
@@ -187,21 +187,32 @@
 
 
 def step_kernel(
-    seg_count, ep_count, heads, dim, tile,
+    seg_count, ep_count, heads, dim, tile, wide, lags,
     q_ref, k_ref, v_ref, proj_hbm, up_hbm, down_hbm,
-    decay_ref, turned_ref, experts_ref, gates_ref, gain_ref,
+    turned_ref, experts_ref, gates_ref, gain_ref,
     attn_ref, out_ref,
     qb, kb, vb, states, ends, table_ref, mix_ref,
-    up, down, proj, rows, part, sums, full, acc, hidden, tokens,
+    up, down, proj, rows, part, x_sum, z_part, z_in, full, acc, hidden, tokens,
     terms, core_in, both, y_in, x_in, middle, line, line_in,
     load_sem, in_send, in_recv, gate_send, gate_recv,
     st_send, st_recv, end_send, end_recv, row_send, row_recv, pick_send, pick_recv,
-    rs_send, rs_recv, ag_send, ag_recv, x_send, x_recv, y_send, y_recv, c_send, c_recv,
+    rx_send, rx_recv, rz_send, rz_recv,
+    ag_send, ag_recv, x_send, x_recv, y_send, y_recv, c_send, c_recv,
     t_send, t_recv, tc_send, tc_recv, ty_send, ty_recv, tx_send, tx_recv, tz_send, tz_recv,
 ):
+    f32, bf16 = jnp.float32, jnp.bfloat16
     seg, ep = greet(seg_count, ep_count)
     width = heads * dim
-    tokens_own, moe_own = q_ref.shape[0], experts_ref.shape[0]
+    tokens_own, moe_own = q_ref.shape[0], experts_ref.shape[1]
+    y_count, half = seg_count // 2, ep_count // 2
+    core, y = lax.rem(seg, 2), lax.div(seg, 2)
+    x, z = lax.rem(ep, 2), lax.div(ep, 2)
+    x_mate = ep + 1 - 2 * x
+    mate = seg + 1 - 2 * core
+
+    def seg_at(d, i):
+        return lax.rem(y + d + y_count, y_count) * 2 + (core if i == 0 else 1 - core)
+
     triples = ((k_ref, kb), (v_ref, vb), (q_ref, qb))
     sends = {}
     own = pl.ds(pl.multiple_of(ep * width, width), width)
@@ -226,10 +237,23 @@
     ]
     for load in loads:
         load.start()
-    lanes = lax.broadcasted_iota(jnp.int32, (moe_own, 128), 1)
+    lanes = lax.broadcasted_iota(jnp.int32, (moe_own, 128), 1).astype(f32)
+    corner = (
+        lax.broadcasted_iota(jnp.int32, (moe_own, moe_own), 0)
+        == lax.broadcasted_iota(jnp.int32, (moe_own, moe_own), 1)
+    )
+
+    def upright(line):
+        spread = jnp.broadcast_to(line, (moe_own, moe_own))
+        return jnp.sum(jnp.where(corner, spread, 0.0), axis=1, keepdims=True)
+
     table_ref[seg, ep] = sum(
-        jnp.where(experts_ref[:, i : i + 1] == lanes, gates_ref[:, i : i + 1], 0.0)
-        for i in range(experts_ref.shape[1])
+        jnp.where(
+            upright(experts_ref[i : i + 1, :].astype(f32)) == lanes,
+            upright(gates_ref[i : i + 1, :]),
+            0.0,
+        )
+        for i in range(experts_ref.shape[0])
     )
     gates = []
     for j in range(1, ep_count):
@@ -244,11 +268,15 @@
     rows_at = lax.broadcasted_iota(jnp.int32, (length, length), 0)
     columns_at = lax.broadcasted_iota(jnp.int32, (length, length), 1)
     causal = rows_at >= columns_at
-    lower = causal.astype(jnp.float32)
-    cum = jnp.dot(lower, decay_ref[...], precision=highest, preferred_element_type=jnp.float32)
+    lower = causal.astype(f32)
+    turned_decay = turned_ref[...]
     across = lax.dot_general(
-        turned_ref[...], lower, (((1,), (1,)), ((), ())), precision=highest,
-        preferred_element_type=jnp.float32,
+        turned_decay, lower, (((1,), (1,)), ((), ())), precision=highest,
+        preferred_element_type=f32,
+    )
+    cum = lax.dot_general(
+        lower, turned_decay, (((1,), (1,)), ((), ())), precision=highest,
+        preferred_element_type=f32,
     )
     for copy in keep:
         copy.wait()
@@ -262,26 +290,22 @@
     unit = (
         lax.broadcasted_iota(jnp.int32, (dim, dim), 0)
         == lax.broadcasted_iota(jnp.int32, (dim, dim), 1)
-    ).astype(jnp.float32).astype(jnp.bfloat16)
+    ).astype(f32).astype(bf16)
     for h in range(heads):
         cols = slice(h * dim, (h + 1) * dim)
         to_end = jnp.exp(ending[:, h : h + 1] - across[h : h + 1, :])
         turned = lax.dot_general(
-            unit, keys[:, cols], (((1,), (1,)), ((), ())), preferred_element_type=jnp.float32
+            unit, keys[:, cols], (((1,), (1,)), ((), ())), preferred_element_type=f32
         )
         states[seg, h] = jnp.dot(
-            (turned * to_end).astype(jnp.bfloat16), values[:, cols],
-            preferred_element_type=jnp.float32,
-        ).astype(jnp.bfloat16)
+            (turned * to_end).astype(bf16), values[:, cols],
+            preferred_element_type=f32,
+        ).astype(bf16)
         ends[seg, h : h + 1] = jnp.broadcast_to(ending[:, h : h + 1], (1, dim))
-    for copy in gates:
-        copy.wait()
     moved = []
     for k in range(1, seg_count):
         other = lax.rem(seg + k, seg_count)
-        for buf, send, recv in (
-            (states, st_send, st_recv), (ends, end_send, end_recv), (table_ref, row_send, row_recv)
-        ):
+        for buf, send, recv in ((states, st_send, st_recv), (ends, end_send, end_recv)):
             copy = remote(buf.at[seg], buf.at[seg], send.at[k], recv.at[k], seg=other)
             copy.start()
             moved.append(copy)
@@ -295,12 +319,12 @@
         weight = jnp.where(causal, jnp.exp(jnp.where(causal, gap, 0.0)), 0.0)
         scores = lax.dot_general(
             queries[:, cols], keys[:, cols], (((1,), (1,)), ((), ())),
-            preferred_element_type=jnp.float32,
+            preferred_element_type=f32,
         )
         inside.append(
             jnp.dot(
-                (scores * weight).astype(jnp.bfloat16), values[:, cols],
-                preferred_element_type=jnp.float32,
+                (scores * weight).astype(bf16), values[:, cols],
+                preferred_element_type=f32,
             )
         )
     for copy in moved:
@@ -308,14 +332,14 @@
     outs = []
     for h in range(heads):
         cols = slice(h * dim, (h + 1) * dim)
-        carried = jnp.zeros((dim, dim), jnp.float32)
+        carried = jnp.zeros((dim, dim), f32)
         for c in range(seg_count):
-            joined = jnp.exp(ends[c, h : h + 1]) * carried + states[c, h].astype(jnp.float32)
+            joined = jnp.exp(ends[c, h : h + 1]) * carried + states[c, h].astype(f32)
             carried = jnp.where(c < seg, joined, carried)
         outside = jnp.exp(cum[:, h : h + 1]) * jnp.dot(
-            queries[:, cols], carried.astype(jnp.bfloat16), preferred_element_type=jnp.float32
-        )
-        outs.append((inside[h] + outside).astype(jnp.bfloat16))
+            queries[:, cols], carried.astype(bf16), preferred_element_type=f32
+        )
+        outs.append((inside[h] + outside).astype(bf16))
     mixture = jnp.concatenate(outs, axis=1)
     mix_ref[...] = mixture.reshape(mix_ref.shape)
     count = length // tokens_own * moe_own
@@ -325,58 +349,104 @@
         == stride * lax.broadcasted_iota(jnp.int32, (count, length), 0)
     )
     rows[seg] = jnp.dot(
-        pick.astype(jnp.float32).astype(jnp.bfloat16), mixture, preferred_element_type=jnp.float32
-    ).astype(jnp.bfloat16)
-    f32, bf16 = jnp.float32, jnp.bfloat16
-    y_count = seg_count // 2
-    core, y = lax.rem(seg, 2), lax.div(seg, 2)
-    mate = seg + 1 - 2 * core
+        pick.astype(f32).astype(bf16), mixture, preferred_element_type=f32
+    ).astype(bf16)
     own_rows = rows.shape[1]
     total = own_rows * seg_count
-    chunk = total // ep_count
+    mine = own_rows // ep_count
     cols = proj.shape[1]
-    moved = []
+    features = width * ep_count
+    sources = [(d, i) for d in range(y_count) for i in range(2)]
+    row_moves = {}
+    for d, i in sources[1:]:
+        row_moves[d, i] = remote(
+            rows.at[seg], rows.at[seg], pick_send.at[d, i], pick_recv.at[d, i], seg=seg_at(d, i)
+        )
+        row_moves[d, i].start()
+    lane = lax.broadcasted_iota(jnp.int32, (own_rows, 128), 1)
+    pieces = {n: [(0, cols + 128)] for n in range(seg_count)}
+    pieces[0] = [(t, tile) for t in range(0, cols - tile, tile)] + [(cols - tile, tile + 128)]
+    x_moves, z_moves = {}, {}
+
+    def source(n):
+        d, i = sources[n]
+        return seg_at(-d, i)
+
+    def project(n):
+        if n:
+            row_moves[sources[n]].wait_recv()
+        picked = rows[source(n)].astype(f32)
+        squares = jnp.sum(picked * picked, axis=1, keepdims=True)
+        high = squares.astype(bf16).astype(f32)
+        pair = jnp.where(lane < 64, high, squares - high).reshape(half, 2, mine, 128).astype(bf16)
+        scaled = (picked * gain_ref[:, own]).astype(bf16)
+        for i in range(2):
+            part[n, i, :, :, cols:] = pair[:, i]
+        for p, (at, size) in enumerate(pieces[n]):
+            for t in range(at, min(at + size, cols), tile):
+                value = (
+                    jnp.dot(scaled, proj[:, t : t + tile], preferred_element_type=f32)
+                    .reshape(half, 2, mine, tile)
+                    .astype(bf16)
+                )
+                for i in range(2):
+                    part[n, i, :, :, t : t + tile] = value[:, i]
+            span = pl.ds(at, size)
+            x_moves[n, p] = remote(
+                part.at[n, 1 - x, :, :, span], x_sum.at[n, :, :, span],
+                rx_send.at[n, p], rx_recv.at[n, p], ep=x_mate,
+            )
+            x_moves[n, p].start()
+
+    def combine(n):
+        for p, (at, size) in enumerate(pieces[n]):
+            x_moves[n, p].wait_recv()
+            span = pl.ds(at, size)
+            value = part[n, x, :, :, span].astype(f32) + x_sum[n, :, :, span].astype(f32)
+            z_part[n, :, :, span] = value.astype(bf16)
+            if at + size > cols:
+                pair = value[:, :, size - 128 :].reshape(half * mine, 128)
+                squares = pair[:, :1] + pair[:, 64:65]
+                high = squares.astype(bf16).astype(f32)
+                pair = jnp.where(lane[: half * mine] < 64, high, squares - high).astype(bf16)
+                z_part[n, :, :, cols:] = pair.reshape(half, mine, 128)
+            for k in range(1, half):
+                other = lax.rem(z + k, half)
+                z_moves[n, p, k] = remote(
+                    z_part.at[n, other, :, span], z_in.at[n, k, :, span],
+                    rz_send.at[n, p, k], rz_recv.at[n, p, k], ep=other * 2 + x,
+                )
+                z_moves[n, p, k].start()
+
+    def finish(n):
+        value = z_part[n, z].astype(f32)
+        for k in range(1, half):
+            for p in range(len(pieces[n])):
+                z_moves[n, p, k].wait_recv()
+            value = value + z_in[n, k].astype(f32)
+        square = value[:, cols : cols + 1] + value[:, cols + 64 : cols + 65]
+        inv_rms = lax.rsqrt(square / features + epsilon)
+        full[seg, source(n), ep] = (value[:, :cols] * inv_rms).astype(bf16)
+
+    loads[0].wait()
+    project(0)
+    for copy in gates:
+        copy.wait()
+    table_moves = []
     for k in range(1, seg_count):
         copy = remote(
-            rows.at[seg], rows.at[seg], pick_send.at[k], pick_recv.at[k],
+            table_ref.at[seg], table_ref.at[seg], row_send.at[k], row_recv.at[k],
             seg=lax.rem(seg + k, seg_count),
         )
         copy.start()
-        moved.append(copy)
-    for copy in moved:
-        copy.wait()
-    picked = rows[...].reshape(total, width).astype(f32)
-    squares = jnp.sum(picked * picked, axis=1, keepdims=True)
-    high = squares.astype(bf16).astype(f32)
-    lane = lax.broadcasted_iota(jnp.int32, (total, 128), 1)
-    pair = jnp.where(lane < 64, high, squares - high).astype(bf16)
-    part[:, :, cols:] = pair.reshape(ep_count, chunk, 128)
-    scaled = (picked * gain_ref[:, own]).astype(bf16)
-    loads[0].wait()
-    for n in range(0, cols, tile):
-        part[:, :, n : n + tile] = (
-            jnp.dot(scaled, proj[:, n : n + tile], preferred_element_type=f32)
-            .astype(bf16)
-            .reshape(ep_count, chunk, tile)
-        )
-    moved = []
-    for j in range(1, ep_count):
-        other = lax.rem(ep + j, ep_count)
-        copy = remote(part.at[other], sums.at[j], rs_send.at[j], rs_recv.at[j], ep=other)
-        copy.start()
-        moved.append(copy)
-    summed = part[ep].astype(f32)
-    for j, copy in enumerate(moved):
-        copy.wait()
-        summed = summed + sums[j + 1].astype(f32)
-    features = width * ep_count
-    square = summed[:, cols : cols + 1] + summed[:, cols + 64 : cols + 65]
-    inv_rms = lax.rsqrt(square / features + epsilon)
-    full[seg, ep] = (summed[:, :cols] * inv_rms).astype(bf16)
-    half = ep_count // 2
-    x, z = lax.rem(ep, 2), lax.div(ep, 2)
-    x_mate = ep + 1 - 2 * x
-    flying = []
+        table_moves.append(copy)
+    for n in range(1, seg_count):
+        project(n)
+        combine(n - 1)
+    combine(seg_count - 1)
+    for n in range(seg_count):
+        finish(n)
+    flying = [*row_moves.values(), *x_moves.values(), *z_moves.values()]
 
     def send(place, send_sem, recv_sem, **target):
         copy = remote(place, place, send_sem, recv_sem, **target)
@@ -388,18 +458,18 @@
         return lax.rem(e - 2 * k + ep_count, ep_count)
 
     def y_seg(k):
-        return lax.rem(y + k + y_count, y_count) * 2 + core
+        return seg_at(k, 0)
 
     z_copies = {}
     for k in range(1, half):
         z_copies[k] = send(
-            full.at[seg, ep], ag_send.at[k], ag_recv.at[k], ep=lax.rem(ep + 2 * k, ep_count)
+            full.at[seg, :, ep], ag_send.at[k], ag_recv.at[k], ep=lax.rem(ep + 2 * k, ep_count)
         )
     x_copies, y_copies = {}, {}
     for k in range(half):
         if k > 0:
             z_copies[k].wait_recv()
-        place = full.at[seg, on_line(ep, k)]
+        place = full.at[seg, :, on_line(ep, k)]
         x_copies[k, 0] = send(place, x_send.at[k, 0], x_recv.at[k, 0], ep=x_mate)
         for d in range(1, y_count):
             y_copies[k, 0, d] = send(
@@ -408,7 +478,7 @@
         send(place, c_send.at[k, 0, 0], c_recv.at[k, 0, 0], seg=mate)
     for k in range(half):
         x_copies[k, 0].wait_recv()
-        place = full.at[seg, on_line(x_mate, k)]
+        place = full.at[seg, :, on_line(x_mate, k)]
         if k % 2 == 0:
             for d in range(1, y_count):
                 y_copies[k, 1, d] = send(
@@ -417,7 +487,7 @@
         send(place, c_send.at[k, 1, 0], c_recv.at[k, 1, 0], seg=mate)
         for d in range(1, y_count):
             y_copies[k, 0, d].wait_recv()
-            place = full.at[y_seg(-d), on_line(ep, k)]
+            place = full.at[y_seg(-d), :, on_line(ep, k)]
             if k % 2 == 1:
                 x_copies[k, d] = send(place, x_send.at[k, d], x_recv.at[k, d], ep=x_mate)
             send(place, c_send.at[k, 0, d], c_recv.at[k, 0, d], seg=mate)
@@ -427,7 +497,7 @@
     def multiply(s):
         def step(n, carry):
             at = pl.multiple_of(n * tile, tile)
-            block = full[s, :, :, pl.ds(at, tile)].reshape(total, tile)
+            block = full[s, :, :, :, pl.ds(at, tile)].reshape(total, tile)
             lines = pl.ds(pl.multiple_of(s * cols + n * tile, tile), tile)
             acc[...] += lax.dot_general(
                 block, up[:, lines], (((1,), (1,)), ((), ())), preferred_element_type=f32
@@ -441,7 +511,7 @@
         for d in range(1, y_count):
             (y_copies[k, 1, d] if k % 2 == 0 else x_copies[k, d]).wait_recv()
             send(
-                full.at[y_seg(-d), on_line(x_mate, k)],
+                full.at[y_seg(-d), :, on_line(x_mate, k)],
                 c_send.at[k, 1, d], c_recv.at[k, 1, d], seg=mate,
             )
     for d in range(1, y_count):
@@ -449,7 +519,7 @@
     for k in range(half):
         for i in range(2):
             for d in range(y_count):
-                place = full.at[seg, ep]
+                place = full.at[seg, :, ep]
                 remote(place, place, c_send.at[k, i, d], c_recv.at[k, i, d], seg=mate).wait_recv()
     for copy in flying:
         copy.wait_send()
@@ -461,21 +531,24 @@
         copy.start()
         backs.append(copy)
     for k in range(y_count):
-        multiply(lax.rem(y + k, y_count) * 2 + 1 - core)
+        multiply(seg_at(k, 1))
     value = acc[...]
     hidden[...] = (value / (1.0 + jnp.exp(-value))).astype(bf16)
+    for copy in table_moves:
+        copy.wait()
     table = table_ref[...].reshape(total, 128)
-    gate = jnp.sum(jnp.where(lane == lax.div(ep, 2), table, 0.0), axis=1, keepdims=True)
+    lane = lax.broadcasted_iota(jnp.int32, (total, 128), 1)
+    gate = jnp.sum(jnp.where(lane == z, table, 0.0), axis=1, keepdims=True)
     loads[2].wait()
-    steps = seg_count
+    steps = seg_count * cols // wide
     core_moves = {}
 
     def product(c):
-        for n in range(0, cols, tile):
-            at = c * cols + n
-            value = jnp.dot(hidden[...], down[:, at : at + tile], preferred_element_type=f32)
-            value = jnp.where(gate != 0.0, value * gate, 0.0).astype(bf16)
-            terms[c, :, :, n : n + tile] = value.reshape(seg_count, own_rows, tile)
+        value = jnp.dot(
+            hidden[...], down[:, c * wide : (c + 1) * wide], preferred_element_type=f32
+        )
+        value = jnp.where(gate != 0.0, value * gate, 0.0).astype(bf16)
+        terms[c] = value.reshape(seg_count, own_rows, wide)
         core_moves[c] = []
         for k in range(y_count):
             copy = remote(
@@ -486,14 +559,13 @@
             core_moves[c].append(copy)
 
     first, second, last = {}, {}, {}
-    mine = own_rows // ep_count
 
     def joined(c):
         for copy in core_moves[c]:
             copy.wait()
         for k in range(y_count):
             value = (terms[c, k * 2 + core].astype(f32) + core_in[c, k].astype(f32)).reshape(
-                half, 2, mine, cols
+                half, 2, mine, wide
             ).astype(bf16)
             for i in range(2):
                 both[c, k, i] = value[:, i]
@@ -563,29 +635,32 @@
             copy.start()
             last[c].append(copy)
 
-    for c in range(steps + 3):
+    def settle():
+        for copy in backs:
+            copy.wait()
+        mixed = [tokens[p].astype(f32) for p in range(ep_count)]
+        square = sum(jnp.sum(m * m, axis=1, keepdims=True) for m in mixed)
+        inv_rms = lax.rsqrt(square / features + epsilon)
+        for p in range(ep_count):
+            at = slice(p * width, (p + 1) * width)
+            attn_ref[:, at] = (mixed[p] * inv_rms * gain_ref[:, at]).astype(bf16)
+
+    for c in range(steps + lags[2]):
         if c < steps:
             product(c)
-        if 0 <= c - 1 < steps:
-            joined(c - 1)
-        if 0 <= c - 2 < steps:
-            crossed(c - 2)
-        if 0 <= c - 3 < steps:
-            along(c - 3)
-    for copy in backs:
-        copy.wait()
-    mixed = [tokens[p].astype(f32) for p in range(ep_count)]
-    square = sum(jnp.sum(m * m, axis=1, keepdims=True) for m in mixed)
-    inv_rms = lax.rsqrt(square / features + epsilon)
-    for p in range(ep_count):
-        at = slice(p * width, (p + 1) * width)
-        attn_ref[:, at] = (mixed[p] * inv_rms * gain_ref[:, at]).astype(bf16)
+        if 0 <= c - lags[0] < steps:
+            joined(c - lags[0])
+        if 0 <= c - lags[1] < steps:
+            crossed(c - lags[1])
+        if 0 <= c - lags[2] < steps:
+            along(c - lags[2])
+    settle()
     for c in range(steps):
         value = line[c, z].astype(f32)
         for j, copy in enumerate(last[c]):
             copy.wait()
             value = value + line_in[c, j + 1].astype(f32)
-        out_ref[:, c * cols : (c + 1) * cols] = value.astype(bf16)
+        out_ref[:, c * wide : (c + 1) * wide] = value.astype(bf16)
 
 
 def on_device_dense(
@@ -604,16 +679,18 @@
     total = seg_rows * seg_count
     cols = out_proj.shape[1]
     model, units = up_weight.shape[1:]
-    chunk = total // ep_count
+    tile = math.gcd(cols, 512)
+    wide = tile
+    steps = model // wide
     vmem = pl.BlockSpec(memory_space=pltpu.VMEM)
     hbm = pl.BlockSpec(memory_space=pl.ANY)
     return pl.pallas_call(
-        functools.partial(step_kernel, seg_count, ep_count, heads, dim, math.gcd(cols, 512)),
+        functools.partial(step_kernel, seg_count, ep_count, heads, dim, tile, wide, (1, 3, 5)),
         out_shape=(
             jax.ShapeDtypeStruct((tokens_own, features), bf16),
             jax.ShapeDtypeStruct((moe_own, model), bf16),
         ),
-        in_specs=[hbm] * 6 + [vmem] * 5,
+        in_specs=[hbm] * 6 + [vmem] * 4,
         out_specs=(vmem, vmem),
         scratch_shapes=[VM((ep_count, tokens_own, width), bf16)] * 3
         + [
@@ -625,39 +702,43 @@
             VM((units, model), bf16),
             VM((width, cols), bf16),
             VM((seg_count, seg_rows, width), bf16),
-            VM((ep_count, chunk, cols + 128), bf16),
-            VM((ep_count, chunk, cols + 128), bf16),
-            VM((seg_count, ep_count, chunk, cols), bf16),
+            VM((seg_count, 2, half, moe_own, cols + 128), bf16),
+            VM((seg_count, half, moe_own, cols + 128), bf16),
+            VM((seg_count, half, moe_own, cols + 128), bf16),
+            VM((seg_count, half, moe_own, cols + 128), bf16),
+            VM((seg_count, seg_count, ep_count, moe_own, cols), bf16),
             VM((total, units), f32),
             VM((total, units), bf16),
             VM((ep_count, tokens_own, width), bf16),
-            VM((seg_count, seg_count, seg_rows, cols), bf16),
-            VM((seg_count, y_count, seg_rows, cols), bf16),
-            VM((seg_count, y_count, 2, half, moe_own, cols), bf16),
-            VM((seg_count, y_count, 2, half, moe_own, cols), bf16),
-            VM((seg_count, y_count, half, moe_own, cols), bf16),
-            VM((seg_count, max(2, y_count), half, moe_own, cols), bf16),
-            VM((seg_count, half, moe_own, cols), bf16),
-            VM((seg_count, half, moe_own, cols), bf16),
+            VM((steps, seg_count, seg_rows, wide), bf16),
+            VM((steps, y_count, seg_rows, wide), bf16),
+            VM((steps, y_count, 2, half, moe_own, wide), bf16),
+            VM((steps, y_count, 2, half, moe_own, wide), bf16),
+            VM((steps, y_count, half, moe_own, wide), bf16),
+            VM((steps, max(2, y_count), half, moe_own, wide), bf16),
+            VM((steps, half, moe_own, wide), bf16),
+            VM((steps, half, moe_own, wide), bf16),
             dma((6,)),
         ]
         + [dma((3, ep_count))] * 2
         + [dma((ep_count,))] * 2
-        + [dma((seg_count,))] * 8
-        + [dma((ep_count,))] * 2
+        + [dma((seg_count,))] * 6
+        + [dma((y_count, 2))] * 2
+        + [dma((seg_count, cols // tile))] * 2
+        + [dma((seg_count, cols // tile, half))] * 2
         + [dma((half,))] * 2
         + [dma((half, y_count))] * 2
         + [dma((half, 2, y_count))] * 4
         + [dma((ep_count,))] * 2
-        + [dma((seg_count, y_count))] * 4
-        + [dma((seg_count,))] * 2
-        + [dma((seg_count, half))] * 2,
+        + [dma((steps, y_count))] * 4
+        + [dma((steps,))] * 2
+        + [dma((steps, half))] * 2,
         compiler_params=pltpu.CompilerParams(
             collective_id=1, has_side_effects=True, vmem_limit_bytes=62 * 2**20
         ),
     )(
         queries, keys, values, out_proj, jnp.swapaxes(up_weight, 1, 2), down_weight,
-        log_decay, log_decay.T, experts, gates, out_gain[None, :],
+        log_decay.T, experts.T, gates.T, out_gain[None, :],
     )
 
 

time: 119 us -> 104 us (0.87)
  Pallas kernels: 111 us -> 99.9 us
  local copies, waits for them, and re-layouts: 7.44 us -> 3.21 us
    pallas_call x1, Pallas kernels: 111 us -> 99.9 us  [on_device_dense(): pl.pallas_call(functools.partial(step_kernel, seg_count, ep_count, heads,...]
    unnamed x5 -> x2, local copies, waits for them, and re-layouts: 7.44 us -> 3.21 us
where the time goes in v1:
time: 104 us
  Pallas kernels  99.9 us (96%)
  local copies, waits for them, and re-layouts  3.21 us (3%)
    pallas_call x1, Pallas kernels, on_device_dense(): pl.pallas_call(functools.partial(step_kernel, seg_count, ep_count, heads,...  99.9 us
    unnamed x2, local copies, waits for them, and re-layouts  3.21 us

profile of v1, /device:TPU:0, one launch (start us, length us, event | category | flops | bytes accessed | tf_op | source)
XLA Modules:
  0.0 103.8 jit_solution(6549709489578227592)
XLA Ops:
  0.6 99.9 %shard_map.113 = (bf16[64,2048]{1,0:T(8,128)(2,1)}, bf16[8,6144]{1,0:T(8,128)(2,1)}) custom-call(bf16[64,2048]{1,0:T(8,128)(2,1)} %q_ref.1, bf16[64,2048]{1,0:T(8,128)(2,1)} %k_ref.1, bf16[64,2048]{1,0:T(8,128)(2,1)} %v_ref.1, bf16[256,1536]{1,0:T(8,128)(2,1)} %proj_hbm.1, bf16[1,576,6144]{2,1,0:T(8,128)(2,1)} %bitcast.5, bf16[1,576,6144]{2,1,0:T(8,128)(2,1)} %down_hbm.1, ...), custom_call_target="tpu_custom_call" | custom-call | tf_op jit(solution)/shard_map/pallas_call | solution.py:687
  100.6 1.7 %copy.14 = bf16[64,2048]{1,0:T(8,128)(2,1)} copy(bf16[64,2048]{1,0:T(8,128)(2,1)} %get-tuple-element.4) | data formatting | bytes 524288
  102.3 1.5 %copy.15 = bf16[8,6144]{1,0:T(8,128)(2,1)} copy(bf16[8,6144]{1,0:T(8,128)(2,1)} %get-tuple-element.5) | data formatting | bytes 196608

commit v2 on v1

--- a/solution.py
+++ b/solution.py
@@ -187,20 +187,31 @@
 
 
 def step_kernel(
-    seg_count, ep_count, heads, dim, tile, wide, lags,
+    seg_count, ep_count, heads, dim, tile, wide, lags, by_x,
     q_ref, k_ref, v_ref, proj_hbm, up_hbm, down_hbm,
-    turned_ref, experts_ref, gates_ref, gain_ref,
-    attn_ref, out_ref,
-    qb, kb, vb, states, ends, table_ref, mix_ref,
+    turned_hbm, experts_hbm, gates_hbm, gain_hbm,
+    attn_hbm, out_hbm,
+    turned_ref, experts_ref, gates_ref, gain_ref, attn_ref, out_ref,
+    kvb, qb, q_own, q_out, q_in, states, ends, table_ref, mix_ref,
     up, down, proj, rows, part, x_sum, z_part, z_in, full, acc, hidden, tokens,
     terms, core_in, both, y_in, x_in, middle, line, line_in,
-    load_sem, in_send, in_recv, gate_send, gate_recv,
-    st_send, st_recv, end_send, end_recv, row_send, row_recv, pick_send, pick_recv,
-    rx_send, rx_recv, rz_send, rz_recv,
-    ag_send, ag_recv, x_send, x_recv, y_send, y_recv, c_send, c_recv,
-    t_send, t_recv, tc_send, tc_recv, ty_send, ty_recv, tx_send, tx_recv, tz_send, tz_recv,
+    load_sem, one_send, one_recv, pick_recv, rx_recv, rz_recv,
+    ag_recv, x_recv, y_recv, xy_recv, c_recv, tc_recv, ty_recv, tx_recv, tz_recv,
 ):
     f32, bf16 = jnp.float32, jnp.bfloat16
+    smalls = [
+        pltpu.make_async_copy(src, dst, load_sem.at[4 + i])
+        for i, (src, dst) in enumerate(
+            (
+                (turned_hbm, turned_ref), (experts_hbm, experts_ref), (gates_hbm, gates_ref),
+                (gain_hbm, gain_ref),
+            )
+        )
+    ]
+    early = pltpu.make_async_copy(q_ref, q_own, load_sem.at[3])
+    early.start()
+    for copy in smalls:
+        copy.start()
     seg, ep = greet(seg_count, ep_count)
     width = heads * dim
     tokens_own, moe_own = q_ref.shape[0], experts_ref.shape[1]
@@ -211,25 +222,34 @@
     mate = seg + 1 - 2 * core
 
     def seg_at(d, i):
-        return lax.rem(y + d + y_count, y_count) * 2 + (core if i == 0 else 1 - core)
-
-    triples = ((k_ref, kb), (v_ref, vb), (q_ref, qb))
-    sends = {}
+        return lax.rem(y + d + 2 * y_count, y_count) * 2 + (core if i == 0 else 1 - core)
+
     own = pl.ds(pl.multiple_of(ep * width, width), width)
-    keep = []
-    for i, (ref, buf) in enumerate(triples):
-        sends[i] = []
+    pending = []
+
+    def waiter(ref, recv, **target):
+        return remote(ref, ref, one_send.at[0], recv, **target)
+
+    def collect(ref, recv):
+        waiter(ref, recv, ep=x_mate).wait_recv()
+
+    def later(ref, index):
+        pending.append(remote(ref, ref, one_send.at[index], one_recv.at[0], ep=x_mate))
+
+    def scatter(ref, buf, index):
         for j in range(1, ep_count):
             other = lax.rem(ep + j, ep_count)
             columns = pl.ds(pl.multiple_of(other * width, width), width)
-            copy = remote(
-                ref.at[:, columns], buf.at[ep], in_send.at[i, j], in_recv.at[i, j], ep=other
-            )
-            copy.start()
-            sends[i].append(copy)
-        copy = pltpu.make_async_copy(ref.at[:, own], buf.at[ep], load_sem.at[3 + i])
-        copy.start()
-        keep.append(copy)
+            remote(
+                ref.at[:, columns], buf.at[ep], one_send.at[index], one_recv.at[index], ep=other
+            ).start()
+        pltpu.make_async_copy(ref.at[:, own], buf.at[ep], one_recv.at[index]).start()
+
+    others = pl.ds(1, ep_count - 1)
+    other_segs = pl.ds(1, seg_count - 1)
+    scatter(k_ref, kvb.at[0], 0)
+    scatter(v_ref, kvb.at[1], 0)
+    later(kvb.at[:, others], 0)
     loads = [
         pltpu.make_async_copy(proj_hbm, proj, load_sem.at[0]),
         pltpu.make_async_copy(up_hbm.at[0], up, load_sem.at[1]),
@@ -237,6 +257,24 @@
     ]
     for load in loads:
         load.start()
+    stride = tokens_own // moe_own
+    few = (
+        lax.broadcasted_iota(jnp.int32, (moe_own, tokens_own), 1)
+        == stride * lax.broadcasted_iota(jnp.int32, (moe_own, tokens_own), 0)
+    )
+    early.wait()
+    chosen = jnp.dot(
+        few.astype(f32).astype(bf16), q_own[...], preferred_element_type=f32
+    ).astype(bf16)
+    for p in range(ep_count):
+        q_out[p] = chosen[:, p * width : (p + 1) * width]
+    for j in range(1, ep_count):
+        other = lax.rem(ep + j, ep_count)
+        remote(q_out.at[other], q_in.at[ep], one_send.at[2], one_recv.at[2], ep=other).start()
+    later(q_in.at[others], 2)
+    q_in[ep] = q_out[ep]
+    for copy in smalls:
+        copy.wait()
     lanes = lax.broadcasted_iota(jnp.int32, (moe_own, 128), 1).astype(f32)
     corner = (
         lax.broadcasted_iota(jnp.int32, (moe_own, moe_own), 0)
@@ -255,14 +293,12 @@
         )
         for i in range(experts_ref.shape[0])
     )
-    gates = []
     for j in range(1, ep_count):
-        copy = remote(
-            table_ref.at[seg, ep], table_ref.at[seg, ep], gate_send.at[j], gate_recv.at[j],
+        remote(
+            table_ref.at[seg, ep], table_ref.at[seg, ep], one_send.at[3], one_recv.at[3],
             ep=lax.rem(ep + j, ep_count),
-        )
-        copy.start()
-        gates.append(copy)
+        ).start()
+    later(table_ref.at[0, others], 3)
     length = tokens_own * ep_count
     highest = lax.Precision.HIGHEST
     rows_at = lax.broadcasted_iota(jnp.int32, (length, length), 0)
@@ -278,13 +314,17 @@
         lower, turned_decay, (((1,), (1,)), ((), ())), precision=highest,
         preferred_element_type=f32,
     )
-    for copy in keep:
-        copy.wait()
-    for i in (0, 1):
-        for copy in sends[i]:
-            copy.wait()
+    count = ep_count * moe_own
+    causal_few = lax.broadcasted_iota(
+        jnp.int32, (count, length), 1
+    ) <= stride * lax.broadcasted_iota(jnp.int32, (count, length), 0)
+    cum_few = lax.dot_general(
+        causal_few.astype(f32), turned_decay, (((1,), (1,)), ((), ())), precision=highest,
+        preferred_element_type=f32,
+    )
+    collect(kvb, one_recv.at[0])
     keys, values = (
-        jnp.concatenate([b[p] for p in range(ep_count)], axis=0) for b in (kb, vb)
+        jnp.concatenate([kvb[i, p] for p in range(ep_count)], axis=0) for i in range(2)
     )
     ending = cum[length - 1 : length, :]
     unit = (
@@ -302,55 +342,61 @@
             preferred_element_type=f32,
         ).astype(bf16)
         ends[seg, h : h + 1] = jnp.broadcast_to(ending[:, h : h + 1], (1, dim))
-    moved = []
     for k in range(1, seg_count):
         other = lax.rem(seg + k, seg_count)
-        for buf, send, recv in ((states, st_send, st_recv), (ends, end_send, end_recv)):
-            copy = remote(buf.at[seg], buf.at[seg], send.at[k], recv.at[k], seg=other)
-            copy.start()
-            moved.append(copy)
-    for copy in sends[2]:
-        copy.wait()
-    queries = jnp.concatenate([qb[p] for p in range(ep_count)], axis=0)
-    inside = []
-    for h in range(heads):
+        for buf, index in ((states, 4), (ends, 5)):
+            remote(
+                buf.at[seg], buf.at[seg], one_send.at[index], one_recv.at[index], seg=other
+            ).start()
+    later(states.at[other_segs], 4)
+    later(ends.at[other_segs], 5)
+
+    def within(asked, mask, cum, h):
         cols = slice(h * dim, (h + 1) * dim)
         gap = cum[:, h : h + 1] - across[h : h + 1, :]
-        weight = jnp.where(causal, jnp.exp(jnp.where(causal, gap, 0.0)), 0.0)
+        weight = jnp.where(mask, jnp.exp(jnp.where(mask, gap, 0.0)), 0.0)
         scores = lax.dot_general(
-            queries[:, cols], keys[:, cols], (((1,), (1,)), ((), ())),
+            asked[:, cols], keys[:, cols], (((1,), (1,)), ((), ())),
             preferred_element_type=f32,
         )
-        inside.append(
-            jnp.dot(
-                (scores * weight).astype(bf16), values[:, cols],
-                preferred_element_type=f32,
+        return jnp.dot(
+            (scores * weight).astype(bf16), values[:, cols], preferred_element_type=f32
+        )
+
+    def before(asked, cum, h):
+        cols = slice(h * dim, (h + 1) * dim)
+        return jnp.exp(cum[:, h : h + 1]) * jnp.dot(
+            asked[:, cols], carried[h], preferred_element_type=f32
+        )
+
+    collect(q_in.at[others], one_recv.at[2])
+    asked = q_in[...].reshape(count, width)
+    inside = [within(asked, causal_few, cum_few, h) for h in range(heads)]
+    scatter(q_ref, qb, 1)
+    later(qb.at[others], 1)
+    collect(states.at[other_segs], one_recv.at[4])
+    collect(ends.at[other_segs], one_recv.at[5])
+    carried = []
+    for h in range(heads):
+        joined = jnp.zeros((dim, dim), f32)
+        for c in range(seg_count):
+            after = jnp.exp(ends[c, h : h + 1]) * joined + states[c, h].astype(f32)
+            joined = jnp.where(c < seg, after, joined)
+        carried.append(joined.astype(bf16))
+    for h in range(heads):
+        rows[seg, :, h * dim : (h + 1) * dim] = (
+            inside[h] + before(asked, cum_few, h)
+        ).astype(bf16)
+
+    def mix_all():
+        collect(qb, one_recv.at[1])
+        queries = jnp.concatenate([qb[p] for p in range(ep_count)], axis=0)
+        for h in range(heads):
+            value = within(queries, causal, cum, h) + before(queries, cum, h)
+            mix_ref[:, :, h * dim : (h + 1) * dim] = value.astype(bf16).reshape(
+                ep_count, tokens_own, dim
             )
-        )
-    for copy in moved:
-        copy.wait()
-    outs = []
-    for h in range(heads):
-        cols = slice(h * dim, (h + 1) * dim)
-        carried = jnp.zeros((dim, dim), f32)
-        for c in range(seg_count):
-            joined = jnp.exp(ends[c, h : h + 1]) * carried + states[c, h].astype(f32)
-            carried = jnp.where(c < seg, joined, carried)
-        outside = jnp.exp(cum[:, h : h + 1]) * jnp.dot(
-            queries[:, cols], carried.astype(bf16), preferred_element_type=f32
-        )
-        outs.append((inside[h] + outside).astype(bf16))
-    mixture = jnp.concatenate(outs, axis=1)
-    mix_ref[...] = mixture.reshape(mix_ref.shape)
-    count = length // tokens_own * moe_own
-    stride = length // count
-    pick = (
-        lax.broadcasted_iota(jnp.int32, (count, length), 1)
-        == stride * lax.broadcasted_iota(jnp.int32, (count, length), 0)
-    )
-    rows[seg] = jnp.dot(
-        pick.astype(f32).astype(bf16), mixture, preferred_element_type=f32
-    ).astype(bf16)
+
     own_rows = rows.shape[1]
     total = own_rows * seg_count
     mine = own_rows // ep_count
@@ -360,13 +406,15 @@
     row_moves = {}
     for d, i in sources[1:]:
         row_moves[d, i] = remote(
-            rows.at[seg], rows.at[seg], pick_send.at[d, i], pick_recv.at[d, i], seg=seg_at(d, i)
+            rows.at[seg], rows.at[seg], one_send.at[6], pick_recv.at[d * 2 + i - 1],
+            seg=seg_at(d, i),
         )
         row_moves[d, i].start()
+    later(rows.at[other_segs], 6)
     lane = lax.broadcasted_iota(jnp.int32, (own_rows, 128), 1)
     pieces = {n: [(0, cols + 128)] for n in range(seg_count)}
     pieces[0] = [(t, tile) for t in range(0, cols - tile, tile)] + [(cols - tile, tile + 128)]
-    x_moves, z_moves = {}, {}
+    x_moves = {}
 
     def source(n):
         d, i = sources[n]
@@ -394,7 +442,7 @@
             span = pl.ds(at, size)
             x_moves[n, p] = remote(
                 part.at[n, 1 - x, :, :, span], x_sum.at[n, :, :, span],
-                rx_send.at[n, p], rx_recv.at[n, p], ep=x_mate,
+                one_send.at[7], rx_recv.at[(n + len(pieces[0]) - 1 if n else p)], ep=x_mate,
             )
             x_moves[n, p].start()
 
@@ -412,17 +460,15 @@
                 z_part[n, :, :, cols:] = pair.reshape(half, mine, 128)
             for k in range(1, half):
                 other = lax.rem(z + k, half)
-                z_moves[n, p, k] = remote(
+                remote(
                     z_part.at[n, other, :, span], z_in.at[n, k, :, span],
-                    rz_send.at[n, p, k], rz_recv.at[n, p, k], ep=other * 2 + x,
-                )
-                z_moves[n, p, k].start()
+                    one_send.at[8], rz_recv.at[n], ep=other * 2 + x,
+                ).start()
 
     def finish(n):
+        collect(z_in.at[n, pl.ds(1, half - 1)], rz_recv.at[n])
         value = z_part[n, z].astype(f32)
         for k in range(1, half):
-            for p in range(len(pieces[n])):
-                z_moves[n, p, k].wait_recv()
             value = value + z_in[n, k].astype(f32)
         square = value[:, cols : cols + 1] + value[:, cols + 64 : cols + 65]
         inv_rms = lax.rsqrt(square / features + epsilon)
@@ -430,28 +476,18 @@
 
     loads[0].wait()
     project(0)
-    for copy in gates:
-        copy.wait()
-    table_moves = []
+    later(x_sum, 7)
+    later(z_in.at[:, pl.ds(1, half - 1)], 8)
+    collect(table_ref.at[0, others], one_recv.at[3])
     for k in range(1, seg_count):
-        copy = remote(
-            table_ref.at[seg], table_ref.at[seg], row_send.at[k], row_recv.at[k],
+        remote(
+            table_ref.at[seg], table_ref.at[seg], one_send.at[9], one_recv.at[9],
             seg=lax.rem(seg + k, seg_count),
-        )
+        ).start()
+    later(table_ref.at[other_segs], 9)
+    def send(place, index, recv_sem, **target):
+        copy = remote(place, place, one_send.at[index], recv_sem, **target)
         copy.start()
-        table_moves.append(copy)
-    for n in range(1, seg_count):
-        project(n)
-        combine(n - 1)
-    combine(seg_count - 1)
-    for n in range(seg_count):
-        finish(n)
-    flying = [*row_moves.values(), *x_moves.values(), *z_moves.values()]
-
-    def send(place, send_sem, recv_sem, **target):
-        copy = remote(place, place, send_sem, recv_sem, **target)
-        copy.start()
-        flying.append(copy)
         return copy
 
     def on_line(e, k):
@@ -460,37 +496,80 @@
     def y_seg(k):
         return seg_at(k, 0)
 
-    z_copies = {}
-    for k in range(1, half):
-        z_copies[k] = send(
-            full.at[seg, :, ep], ag_send.at[k], ag_recv.at[k], ep=lax.rem(ep + 2 * k, ep_count)
-        )
-    x_copies, y_copies = {}, {}
-    for k in range(half):
+    def block(n, d, e):
+        at, i = sources[n]
+        return full.at[y_seg(-d), seg_at(-d - at, i), e]
+
+    z_copies, x_copies, y_copies = {}, {}, {}
+
+    def spread(n, k):
         if k > 0:
-            z_copies[k].wait_recv()
-        place = full.at[seg, :, on_line(ep, k)]
-        x_copies[k, 0] = send(place, x_send.at[k, 0], x_recv.at[k, 0], ep=x_mate)
+            z_copies[n, k].wait_recv()
+        place = block(n, 0, on_line(ep, k))
+        x_copies[n, k] = send(place, 11, x_recv.at[n, k], ep=x_mate)
         for d in range(1, y_count):
-            y_copies[k, 0, d] = send(
-                place, y_send.at[k, 0, d], y_recv.at[k, 0, d], seg=y_seg(d)
+            y_copies[n, k, d] = send(place, 12, y_recv.at[n, k, d - 1], seg=y_seg(d))
+        send(place, 15, c_recv.at[0], seg=mate)
+
+    def gather_z(n):
+        for k in range(1, half):
+            z_copies[n, k] = send(
+                block(n, 0, ep), 10, ag_recv.at[n, k - 1], ep=lax.rem(ep + 2 * k, ep_count)
             )
-        send(place, c_send.at[k, 0, 0], c_recv.at[k, 0, 0], seg=mate)
-    for k in range(half):
-        x_copies[k, 0].wait_recv()
-        place = full.at[seg, :, on_line(x_mate, k)]
-        if k % 2 == 0:
+        spread(n, 0)
+
+    def gather_xy(n):
+        for k in range(1, half):
+            spread(n, k)
+
+    def relay(n):
+        for k in range(half):
+            x_copies[n, k].wait_recv()
+            place = block(n, 0, on_line(x_mate, k))
+            if k not in by_x:
+                for d in range(1, y_count):
+                    send(place, 13, xy_recv.at[n, 0], seg=y_seg(d))
+            send(place, 15, c_recv.at[0], seg=mate)
             for d in range(1, y_count):
-                y_copies[k, 1, d] = send(
-                    place, y_send.at[k, 1, d], y_recv.at[k, 1, d], seg=y_seg(d)
-                )
-        send(place, c_send.at[k, 1, 0], c_recv.at[k, 1, 0], seg=mate)
-        for d in range(1, y_count):
-            y_copies[k, 0, d].wait_recv()
-            place = full.at[y_seg(-d), :, on_line(ep, k)]
-            if k % 2 == 1:
-                x_copies[k, d] = send(place, x_send.at[k, d], x_recv.at[k, d], ep=x_mate)
-            send(place, c_send.at[k, 0, d], c_recv.at[k, 0, d], seg=mate)
+                y_copies[n, k, d].wait_recv()
+                place = block(n, d, on_line(ep, k))
+                if k in by_x:
+                    send(place, 14, xy_recv.at[n, 1], ep=x_mate)
+                send(place, 15, c_recv.at[d], seg=mate)
+
+    by_y = [k for k in range(half) if k not in by_x]
+
+    def blocks(count):
+        return full.at[0, 0, pl.ds(0, count)]
+
+    def hand_over(n):
+        for i, ks in enumerate((by_y, by_x)):
+            if ks and y_count > 1:
+                collect(blocks(len(ks) * (y_count - 1)), xy_recv.at[n, i])
+            for k in ks:
+                for d in range(1, y_count):
+                    send(block(n, d, on_line(x_mate, k)), 15, c_recv.at[d], seg=mate)
+
+    later(full.at[0, :, pl.ds(0, half - 1)], 10)
+    later(full.at[0, :, pl.ds(0, half)], 11)
+    if y_count > 1:
+        later(full.at[0, :, pl.ds(0, half * (y_count - 1))], 12)
+        for i, ks in enumerate((by_y, by_x)):
+            if ks:
+                later(full.at[0, :, pl.ds(0, len(ks) * (y_count - 1))], 13 + i)
+    later(full.at[pl.ds(0, y_count)], 15)
+
+    def attend():
+        mix_all()
+
+    for stage, n in (
+        (project, 1), (combine, 0), (project, 2), (project, 3), (combine, 1), (attend, None),
+        (combine, 2), (finish, 0), (gather_z, 0), (combine, 3), (finish, 1), (gather_z, 1),
+        (gather_xy, 0), (finish, 2), (gather_z, 2), (gather_xy, 1), (relay, 0),
+        (finish, 3), (gather_z, 3), (gather_xy, 2), (relay, 1), (gather_xy, 3), (hand_over, 0),
+        (relay, 2), (hand_over, 1), (relay, 3),
+    ):
+        stage(*([] if n is None else [n]))
     loads[1].wait()
     acc[...] = jnp.zeros_like(acc)
 
@@ -507,35 +586,23 @@
         lax.fori_loop(0, cols // tile, step, 0)
 
     multiply(seg)
-    for k in range(half):
-        for d in range(1, y_count):
-            (y_copies[k, 1, d] if k % 2 == 0 else x_copies[k, d]).wait_recv()
-            send(
-                full.at[y_seg(-d), :, on_line(x_mate, k)],
-                c_send.at[k, 1, d], c_recv.at[k, 1, d], seg=mate,
-            )
+    for n in range(2, seg_count):
+        hand_over(n)
     for d in range(1, y_count):
         multiply(y_seg(-d))
-    for k in range(half):
-        for i in range(2):
-            for d in range(y_count):
-                place = full.at[seg, :, ep]
-                remote(place, place, c_send.at[k, i, d], c_recv.at[k, i, d], seg=mate).wait_recv()
-    for copy in flying:
-        copy.wait_send()
-    backs = []
     tokens[ep] = mix_ref[ep]
     for j in range(1, ep_count):
         other = lax.rem(ep + j, ep_count)
-        copy = remote(mix_ref.at[other], tokens.at[ep], t_send.at[j], t_recv.at[j], ep=other)
-        copy.start()
-        backs.append(copy)
+        remote(
+            mix_ref.at[other], tokens.at[ep], one_send.at[16], one_recv.at[16], ep=other
+        ).start()
+    later(tokens.at[others], 16)
     for k in range(y_count):
-        multiply(seg_at(k, 1))
+        waiter(full.at[0], c_recv.at[k], seg=mate).wait_recv()
+        multiply(seg_at(-k, 1))
     value = acc[...]
     hidden[...] = (value / (1.0 + jnp.exp(-value))).astype(bf16)
-    for copy in table_moves:
-        copy.wait()
+    collect(table_ref.at[other_segs], one_recv.at[9])
     table = table_ref[...].reshape(total, 128)
     lane = lax.broadcasted_iota(jnp.int32, (total, 128), 1)
     gate = jnp.sum(jnp.where(lane == z, table, 0.0), axis=1, keepdims=True)
@@ -548,103 +615,91 @@
             hidden[...], down[:, c * wide : (c + 1) * wide], preferred_element_type=f32
         )
         value = jnp.where(gate != 0.0, value * gate, 0.0).astype(bf16)
-        terms[c] = value.reshape(seg_count, own_rows, wide)
-        core_moves[c] = []
+        terms[c] = value.reshape(y_count, 2, own_rows, wide)
+        remote(
+            terms.at[c, :, 1 - core], core_in.at[c], one_send.at[17], tc_recv.at[c], seg=mate
+        ).start()
+
+    later(core_in, 17)
+    def joined(c):
+        waiter(core_in.at[c], tc_recv.at[c], seg=mate).wait_recv()
         for k in range(y_count):
-            copy = remote(
-                terms.at[c, k * 2 + 1 - core], core_in.at[c, k],
-                tc_send.at[c, k], tc_recv.at[c, k], seg=mate,
-            )
-            copy.start()
-            core_moves[c].append(copy)
-
-    first, second, last = {}, {}, {}
-
-    def joined(c):
-        for copy in core_moves[c]:
-            copy.wait()
-        for k in range(y_count):
-            value = (terms[c, k * 2 + core].astype(f32) + core_in[c, k].astype(f32)).reshape(
+            value = (terms[c, k, core].astype(f32) + core_in[c, k].astype(f32)).reshape(
                 half, 2, mine, wide
             ).astype(bf16)
             for i in range(2):
                 both[c, k, i] = value[:, i]
-        first[c] = []
         if c % 2 == 0:
             for d in range(1, y_count):
-                first[c].append(
-                    remote(
-                        both.at[c, lax.rem(y + d, y_count)], y_in.at[c, d],
-                        ty_send.at[c, d], ty_recv.at[c, d], seg=y_seg(d),
-                    )
-                )
+                remote(
+                    both.at[c, lax.rem(y + d, y_count)], y_in.at[c, d],
+                    one_send.at[18], ty_recv.at[c], seg=y_seg(d),
+                ).start()
         else:
-            first[c].append(
-                remote(
-                    both.at[c, :, 1 - x], x_in.at[c], tx_send.at[c], tx_recv.at[c], ep=x_mate
-                )
-            )
-        for copy in first[c]:
-            copy.start()
+            remote(
+                both.at[c, :, 1 - x], x_in.at[c, pl.ds(0, y_count)], one_send.at[19],
+                tx_recv.at[c], ep=x_mate,
+            ).start()
+
+    other_ys = pl.ds(1, y_count - 1)
+    evens, odds = pl.ds(0, (steps + 1) // 2), pl.ds(0, steps // 2)
+    later(y_in.at[evens, other_ys], 18)
+    later(x_in.at[odds, pl.ds(0, y_count)], 19)
 
     def crossed(c):
-        for copy in first[c]:
-            copy.wait()
-        second[c] = []
         if c % 2 == 0:
+            collect(y_in.at[c, other_ys], ty_recv.at[c])
             for i in range(2):
                 value = both[c, y, i].astype(f32)
                 for d in range(1, y_count):
                     value = value + y_in[c, d, i].astype(f32)
                 middle[c, i] = value.astype(bf16)
-            second[c].append(
-                remote(
-                    middle.at[c, 1 - x], x_in.at[c, 0], tx_send.at[c], tx_recv.at[c], ep=x_mate
-                )
-            )
+            remote(
+                middle.at[c, 1 - x], x_in.at[c, 0], one_send.at[20], tx_recv.at[c], ep=x_mate
+            ).start()
         else:
+            collect(x_in.at[c, pl.ds(0, y_count)], tx_recv.at[c])
             for k in range(y_count):
                 middle[c, k] = (both[c, k, x].astype(f32) + x_in[c, k].astype(f32)).astype(bf16)
             for d in range(1, y_count):
-                second[c].append(
-                    remote(
-                        middle.at[c, lax.rem(y + d, y_count)], y_in.at[c, d, 0],
-                        ty_send.at[c, d], ty_recv.at[c, d], seg=y_seg(d),
-                    )
-                )
-        for copy in second[c]:
-            copy.start()
+                remote(
+                    middle.at[c, lax.rem(y + d, y_count)], y_in.at[c, d, 0],
+                    one_send.at[21], ty_recv.at[c], seg=y_seg(d),
+                ).start()
+
+    later(x_in.at[evens, 0], 20)
+    later(y_in.at[odds, other_ys, 0], 21)
 
     def along(c):
-        for copy in second[c]:
-            copy.wait()
         if c % 2 == 0:
+            collect(x_in.at[c, 0], tx_recv.at[c])
             value = middle[c, x].astype(f32) + x_in[c, 0].astype(f32)
         else:
+            collect(y_in.at[c, other_ys, 0], ty_recv.at[c])
             value = middle[c, y].astype(f32)
             for d in range(1, y_count):
                 value = value + y_in[c, d, 0].astype(f32)
         line[c] = value.astype(bf16)
-        last[c] = []
         for k in range(1, half):
             other = lax.rem(z + k, half)
-            copy = remote(
-                line.at[c, other], line_in.at[c, k], tz_send.at[c, k], tz_recv.at[c, k],
+            remote(
+                line.at[c, other], line_in.at[c, k], one_send.at[22], tz_recv.at[c],
                 ep=other * 2 + x,
-            )
-            copy.start()
-            last[c].append(copy)
+            ).start()
+
+    later(line_in.at[:, pl.ds(1, half - 1)], 22)
 
     def settle():
-        for copy in backs:
-            copy.wait()
+        collect(tokens.at[others], one_recv.at[16])
         mixed = [tokens[p].astype(f32) for p in range(ep_count)]
         square = sum(jnp.sum(m * m, axis=1, keepdims=True) for m in mixed)
         inv_rms = lax.rsqrt(square / features + epsilon)
         for p in range(ep_count):
             at = slice(p * width, (p + 1) * width)
             attn_ref[:, at] = (mixed[p] * inv_rms * gain_ref[:, at]).astype(bf16)
-
+        result.start()
+
+    result = pltpu.make_async_copy(attn_ref, attn_hbm, load_sem.at[8])
     for c in range(steps + lags[2]):
         if c < steps:
             product(c)
@@ -657,10 +712,34 @@
     settle()
     for c in range(steps):
         value = line[c, z].astype(f32)
-        for j, copy in enumerate(last[c]):
-            copy.wait()
-            value = value + line_in[c, j + 1].astype(f32)
+        collect(line_in.at[c, pl.ds(1, half - 1)], tz_recv.at[c])
+        for k in range(1, half):
+            value = value + line_in[c, k].astype(f32)
         out_ref[:, c * wide : (c + 1) * wide] = value.astype(bf16)
+    whole = pltpu.make_async_copy(out_ref, out_hbm, load_sem.at[9])
+    whole.start()
+    for copy in pending:
+        copy.wait_send()
+    result.wait()
+    whole.wait()
+
+
+def carry_kernel(a_in, b_in, a_out, b_out, a_held, b_held, sem):
+    inward = [
+        pltpu.make_async_copy(src, held, sem.at[0, i])
+        for i, (src, held) in enumerate(((a_in, a_held), (b_in, b_held)))
+    ]
+    outward = [
+        pltpu.make_async_copy(held, dst, sem.at[1, i])
+        for i, (held, dst) in enumerate(((a_held, a_out), (b_held, b_out)))
+    ]
+    for copy in inward:
+        copy.start()
+    for copy, after in zip(inward, outward):
+        copy.wait()
+        after.start()
+    for copy in outward:
+        copy.wait()
 
 
 def on_device_dense(
@@ -682,18 +761,27 @@
     tile = math.gcd(cols, 512)
     wide = tile
     steps = model // wide
-    vmem = pl.BlockSpec(memory_space=pltpu.VMEM)
     hbm = pl.BlockSpec(memory_space=pl.ANY)
-    return pl.pallas_call(
-        functools.partial(step_kernel, seg_count, ep_count, heads, dim, tile, wide, (1, 3, 5)),
+    results = pl.pallas_call(
+        functools.partial(step_kernel, seg_count, ep_count, heads, dim, tile, wide, (1, 6, 11), tuple(range(1, half, 2))),
         out_shape=(
             jax.ShapeDtypeStruct((tokens_own, features), bf16),
             jax.ShapeDtypeStruct((moe_own, model), bf16),
         ),
-        in_specs=[hbm] * 6 + [vmem] * 4,
-        out_specs=(vmem, vmem),
-        scratch_shapes=[VM((ep_count, tokens_own, width), bf16)] * 3
-        + [
+        in_specs=[hbm] * 10,
+        out_specs=(hbm, hbm),
+        scratch_shapes=[
+            VM((heads, log_decay.shape[0]), f32),
+            VM((experts.shape[1], moe_own), jnp.int32),
+            VM((experts.shape[1], moe_own), f32),
+            VM((1, features), f32),
+            VM((tokens_own, features), bf16),
+            VM((moe_own, model), bf16),
+            VM((2, ep_count, tokens_own, width), bf16),
+            VM((ep_count, tokens_own, width), bf16),
+            VM((tokens_own, features), bf16),
+            VM((ep_count, moe_own, width), bf16),
+            VM((ep_count, moe_own, width), bf16),
             VM((seg_count, heads, dim, dim), bf16),
             VM((seg_count, 8, dim), f32),
             VM((seg_count, ep_count, moe_own, 128), f32),
@@ -710,29 +798,27 @@
             VM((total, units), f32),
             VM((total, units), bf16),
             VM((ep_count, tokens_own, width), bf16),
-            VM((steps, seg_count, seg_rows, wide), bf16),
+            VM((steps, y_count, 2, seg_rows, wide), bf16),
             VM((steps, y_count, seg_rows, wide), bf16),
             VM((steps, y_count, 2, half, moe_own, wide), bf16),
             VM((steps, y_count, 2, half, moe_own, wide), bf16),
-            VM((steps, y_count, half, moe_own, wide), bf16),
+            VM((steps, max(2, y_count), half, moe_own, wide), bf16),
             VM((steps, max(2, y_count), half, moe_own, wide), bf16),
             VM((steps, half, moe_own, wide), bf16),
             VM((steps, half, moe_own, wide), bf16),
-            dma((6,)),
+            dma((10,)),
+            dma((23,)),
+            dma((17,)),
+            dma((seg_count - 1,)),
+            dma((seg_count - 1 + cols // tile,)),
+            dma((seg_count,)),
+            dma((seg_count, half - 1)),
+            dma((seg_count, half)),
+            dma((seg_count, half, max(1, y_count - 1))),
+            dma((seg_count, 2)),
+            dma((y_count,)),
         ]
-        + [dma((3, ep_count))] * 2
-        + [dma((ep_count,))] * 2
-        + [dma((seg_count,))] * 6
-        + [dma((y_count, 2))] * 2
-        + [dma((seg_count, cols // tile))] * 2
-        + [dma((seg_count, cols // tile, half))] * 2
-        + [dma((half,))] * 2
-        + [dma((half, y_count))] * 2
-        + [dma((half, 2, y_count))] * 4
-        + [dma((ep_count,))] * 2
-        + [dma((steps, y_count))] * 4
-        + [dma((steps,))] * 2
-        + [dma((steps, half))] * 2,
+        + [dma((steps,))] * 4,
         compiler_params=pltpu.CompilerParams(
             collective_id=1, has_side_effects=True, vmem_limit_bytes=62 * 2**20
         ),
@@ -740,6 +826,13 @@
         queries, keys, values, out_proj, jnp.swapaxes(up_weight, 1, 2), down_weight,
         log_decay.T, experts.T, gates.T, out_gain[None, :],
     )
+    return pl.pallas_call(
+        carry_kernel,
+        out_shape=tuple(jax.ShapeDtypeStruct(r.shape, r.dtype) for r in results),
+        in_specs=[hbm] * 2,
+        out_specs=(hbm, hbm),
+        scratch_shapes=[VM(r.shape, r.dtype) for r in results] + [dma((2, 2))],
+    )(*results)
 
 
 def on_device(*args):

time: 104 us -> 88.8 us (0.85)
  Pallas kernels: 99.9 us -> 88 us
  local copies, waits for them, and re-layouts: 3.21 us -> 0 us
    pallas_call x1, Pallas kernels: 99.9 us -> 86.3 us  [on_device_dense(): pl.pallas_call(functools.partial(step_kernel, seg_count, ep_count, heads,...]
    unnamed x2 -> x0, local copies, waits for them, and re-layouts: 3.21 us -> none
    pallas_call x0 -> x1, Pallas kernels: none -> 1.71 us  [on_device_dense(): pl.pallas_call(carry_kernel, out_shape=tuple((jax.ShapeDtypeStruct(r.shap...]
where the time goes in v2:
time: 88.8 us; the launch traced here: 88.7 us
  Pallas kernels  88 us (99%)
    pallas_call x1, Pallas kernels, on_device_dense(): pl.pallas_call(functools.partial(step_kernel, seg_count, ep_count, heads,...  86.3 us

profile of v2, /device:TPU:0, one launch (start us, length us, event | category | flops | bytes accessed | tf_op | source)
XLA Modules:
  0.0 88.7 jit_solution(11590990428068932333)
XLA Ops:
  0.6 86.3 %shard_map.113 = (bf16[64,2048]{1,0:T(8,128)(2,1)}, bf16[8,6144]{1,0:T(8,128)(2,1)}) custom-call(bf16[64,2048]{1,0:T(8,128)(2,1)} %q_ref.1, bf16[64,2048]{1,0:T(8,128)(2,1)} %k_ref.1, bf16[64,2048]{1,0:T(8,128)(2,1)} %v_ref.1, bf16[256,1536]{1,0:T(8,128)(2,1)} %proj_hbm.1, bf16[1,576,6144]{2,1,0:T(8,128)(2,1)} %bitcast.5, bf16[1,576,6144]{2,1,0:T(8,128)(2,1)} %down_hbm.1, ...), custom_call_target="tpu_custom_call" | custom-call | tf_op jit(solution)/shard_map/pallas_call | solution.py:765
  87.0 1.7 %shard_map.114 = (bf16[64,2048]{1,0:T(8,128)(2,1)}, bf16[8,6144]{1,0:T(8,128)(2,1)}) custom-call(bf16[64,2048]{1,0:T(8,128)(2,1)} %get-tuple-element.4.a_in, bf16[8,6144]{1,0:T(8,128)(2,1)} %get-tuple-element.5.b_in), custom_call_target="tpu_custom_call" | custom-call | tf_op jit(solution)/shard_map/pallas_call | solution.py:829

commit v3 on v2

--- a/solution.py
+++ b/solution.py
@@ -9,6 +9,8 @@
 from jax.sharding import PartitionSpec as P
 
 epsilon = 1e-06
+BYX = (1, 3)
+PACE = ((2.8, 0.71, 3.2, 9.7, 2.5, 3.2, 0.5, 6.0, 11.5), (2.8, 0.71, 3.2, 6.4, 2.5, 3.2, 0.5, 6.0, 13.0))
 MESH = pl.DeviceIdType.MESH
 VM = pltpu.VMEM
 
@@ -187,16 +189,16 @@
 
 
 def step_kernel(
-    seg_count, ep_count, heads, dim, tile, wide, lags, by_x,
+    seg_count, ep_count, heads, dim, tile, wide, lags, by_x, pace,
     q_ref, k_ref, v_ref, proj_hbm, up_hbm, down_hbm,
     turned_hbm, experts_hbm, gates_hbm, gain_hbm,
     attn_hbm, out_hbm,
     turned_ref, experts_ref, gates_ref, gain_ref, attn_ref, out_ref,
     kvb, qb, q_own, q_out, q_in, states, ends, table_ref, mix_ref,
-    up, down, proj, rows, part, x_sum, z_part, z_in, full, acc, hidden, tokens,
+    up, down, proj, rows, part, x_sum, z_part, chain_in, near_out, far_out, scale_ref, full, acc, hidden, tokens,
     terms, core_in, both, y_in, x_in, middle, line, line_in,
-    load_sem, one_send, one_recv, pick_recv, rx_recv, rz_recv,
-    ag_recv, x_recv, y_recv, xy_recv, c_recv, tc_recv, ty_recv, tx_recv, tz_recv,
+    load_sem, one_send, one_recv, pick_recv, rx_recv, chain_recv,
+    x_recv, y_recv, xy_recv, c_recv, tc_recv, ty_recv, tx_recv, tz_recv,
 ):
     f32, bf16 = jnp.float32, jnp.bfloat16
     smalls = [
@@ -220,6 +222,11 @@
     x, z = lax.rem(ep, 2), lax.div(ep, 2)
     x_mate = ep + 1 - 2 * x
     mate = seg + 1 - 2 * core
+
+    nearer = jnp.where(z * 2 < half, 0, 1)
+    at_end = (z == 0) | (z == half - 1)
+    ahead = (z + 1 - 2 * nearer) * 2 + x
+    behind = (z - 1 + 2 * nearer) * 2 + x
 
     def seg_at(d, i):
         return lax.rem(y + d + 2 * y_count, y_count) * 2 + (core if i == 0 else 1 - core)
@@ -412,15 +419,14 @@
         row_moves[d, i].start()
     later(rows.at[other_segs], 6)
     lane = lax.broadcasted_iota(jnp.int32, (own_rows, 128), 1)
-    pieces = {n: [(0, cols + 128)] for n in range(seg_count)}
-    pieces[0] = [(t, tile) for t in range(0, cols - tile, tile)] + [(cols - tile, tile + 128)]
+    pieces = [(0, 128 + tile)] + [(128 + t, tile) for t in range(tile, cols, tile)]
     x_moves = {}
 
     def source(n):
         d, i = sources[n]
         return seg_at(-d, i)
 
-    def project(n):
+    def project(end, n):
         if n:
             row_moves[sources[n]].wait_recv()
         picked = rows[source(n)].astype(f32)
@@ -429,55 +435,91 @@
         pair = jnp.where(lane < 64, high, squares - high).reshape(half, 2, mine, 128).astype(bf16)
         scaled = (picked * gain_ref[:, own]).astype(bf16)
         for i in range(2):
-            part[n, i, :, :, cols:] = pair[:, i]
-        for p, (at, size) in enumerate(pieces[n]):
-            for t in range(at, min(at + size, cols), tile):
-                value = (
-                    jnp.dot(scaled, proj[:, t : t + tile], preferred_element_type=f32)
-                    .reshape(half, 2, mine, tile)
-                    .astype(bf16)
-                )
-                for i in range(2):
-                    part[n, i, :, :, t : t + tile] = value[:, i]
+            part[n, i, :, :, :128] = pair[:, i]
+        for p, (at, size) in enumerate(pieces):
+            t = p * tile
+            value = (
+                jnp.dot(scaled, proj[:, t : t + tile], preferred_element_type=f32)
+                .reshape(half, 2, mine, tile)
+                .astype(bf16)
+            )
+            for i in range(2):
+                part[n, i, :, :, 128 + t : 128 + t + tile] = value[:, i]
             span = pl.ds(at, size)
             x_moves[n, p] = remote(
                 part.at[n, 1 - x, :, :, span], x_sum.at[n, :, :, span],
-                one_send.at[7], rx_recv.at[(n + len(pieces[0]) - 1 if n else p)], ep=x_mate,
+                one_send.at[7], rx_recv.at[n, p], ep=x_mate,
             )
             x_moves[n, p].start()
 
-    def combine(n):
-        for p, (at, size) in enumerate(pieces[n]):
-            x_moves[n, p].wait_recv()
-            span = pl.ds(at, size)
-            value = part[n, x, :, :, span].astype(f32) + x_sum[n, :, :, span].astype(f32)
-            z_part[n, :, :, span] = value.astype(bf16)
-            if at + size > cols:
-                pair = value[:, :, size - 128 :].reshape(half * mine, 128)
-                squares = pair[:, :1] + pair[:, 64:65]
-                high = squares.astype(bf16).astype(f32)
-                pair = jnp.where(lane[: half * mine] < 64, high, squares - high).astype(bf16)
-                z_part[n, :, :, cols:] = pair.reshape(half, mine, 128)
-            for k in range(1, half):
-                other = lax.rem(z + k, half)
-                remote(
-                    z_part.at[n, other, :, span], z_in.at[n, k, :, span],
-                    one_send.at[8], rz_recv.at[n], ep=other * 2 + x,
-                ).start()
-
-    def finish(n):
-        collect(z_in.at[n, pl.ds(1, half - 1)], rz_recv.at[n])
-        value = z_part[n, z].astype(f32)
-        for k in range(1, half):
-            value = value + z_in[n, k].astype(f32)
-        square = value[:, cols : cols + 1] + value[:, cols + 64 : cols + 65]
-        inv_rms = lax.rsqrt(square / features + epsilon)
-        full[seg, source(n), ep] = (value[:, :cols] * inv_rms).astype(bf16)
+    short_lane = lane[: half * mine]
+
+    def keep_sum(ref, n, p, value):
+        at, size = pieces[p]
+        ref[n, :, :, pl.ds(at, size)] = value.astype(bf16)
+        if p == 0:
+            pair = value[:, :, :128].reshape(half * mine, 128)
+            squares = pair[:, :1] + pair[:, 64:65]
+            high = squares.astype(bf16).astype(f32)
+            pair = jnp.where(short_lane < 64, high, squares - high).astype(bf16)
+            ref[n, :, :, :128] = pair.reshape(half, mine, 128)
+
+    def combine(end, n, p):
+        span = pl.ds(*pieces[p])
+        x_moves[n, p].wait_recv()
+        value = part[n, x, :, :, span].astype(f32) + x_sum[n, :, :, span].astype(f32)
+        keep_sum(z_part, n, p, value)
+        if end:
+            remote(
+                z_part.at[n, :, :, span], chain_in.at[nearer, n, :, :, span],
+                one_send.at[8], chain_recv.at[nearer, n, p], ep=ahead,
+            ).start()
+
+    def near(end, n, p):
+        if end:
+            return
+        span = pl.ds(*pieces[p])
+        collect(x_sum.at[n, :, :, span], chain_recv.at[nearer, n, p])
+        value = z_part[n, :, :, span].astype(f32)
+        value = value + chain_in[nearer, n, :, :, span].astype(f32)
+        keep_sum(near_out, n, p, value)
+        remote(
+            near_out.at[n, :, :, span], chain_in.at[nearer, n, :, :, span],
+            one_send.at[8], chain_recv.at[nearer, n, p], ep=ahead,
+        ).start()
+
+    def far(end, n, p):
+        at, size = pieces[p]
+        span = pl.ds(at, size)
+        collect(x_sum.at[n, :, :, span], chain_recv.at[1 - nearer, n, p])
+
+        def settled(value):
+            if p == 0:
+                square = value[:, :, :1] + value[:, :, 64:65]
+                scale_ref[n] = jnp.broadcast_to(
+                    lax.rsqrt(square / features + epsilon), (half, mine, 128)
+                )
+                value = value[:, :, 128:]
+            value = (value * scale_ref[n][:, :, :1]).astype(bf16)
+            start = max(at - 128, 0)
+            for k in range(half):
+                full[seg, source(n), k * 2 + x, :, start : start + tile] = value[k]
+
+        value = z_part[n, :, :, span].astype(f32)
+        value = value + chain_in[1 - nearer, n, :, :, span].astype(f32)
+        if not end:
+            keep_sum(far_out, n, p, value)
+            remote(
+                far_out.at[n, :, :, span], chain_in.at[1 - nearer, n, :, :, span],
+                one_send.at[10], chain_recv.at[1 - nearer, n, p], ep=behind,
+            ).start()
+            value = value + chain_in[nearer, n, :, :, span].astype(f32)
+        settled(value)
 
     loads[0].wait()
-    project(0)
+    project(None, 0)
     later(x_sum, 7)
-    later(z_in.at[:, pl.ds(1, half - 1)], 8)
+    later(x_sum, 8)
     collect(table_ref.at[0, others], one_recv.at[3])
     for k in range(1, seg_count):
         remote(
@@ -491,7 +533,7 @@
         return copy
 
     def on_line(e, k):
-        return lax.rem(e - 2 * k + ep_count, ep_count)
+        return k * 2 + lax.rem(e, 2)
 
     def y_seg(k):
         return seg_at(k, 0)
@@ -500,49 +542,36 @@
         at, i = sources[n]
         return full.at[y_seg(-d), seg_at(-d - at, i), e]
 
-    z_copies, x_copies, y_copies = {}, {}, {}
-
-    def spread(n, k):
-        if k > 0:
-            z_copies[n, k].wait_recv()
-        place = block(n, 0, on_line(ep, k))
-        x_copies[n, k] = send(place, 11, x_recv.at[n, k], ep=x_mate)
+    x_copies, y_copies = {}, {}
+
+    def spread(end, n):
+        for k in range(half):
+            place = block(n, 0, on_line(ep, k))
+            x_copies[n, k] = send(place, 11, x_recv.at[n, k], ep=x_mate)
+            for d in range(1, y_count):
+                y_copies[n, k, d] = send(place, 12, y_recv.at[n, k, d - 1], seg=y_seg(d))
+            send(place, 15, c_recv.at[0], seg=mate)
+
+    def relay(end, n, k):
+        x_copies[n, k].wait_recv()
+        place = block(n, 0, on_line(x_mate, k))
+        if k not in by_x:
+            for d in range(1, y_count):
+                send(place, 13, xy_recv.at[n, 0], seg=y_seg(d))
+        send(place, 15, c_recv.at[0], seg=mate)
         for d in range(1, y_count):
-            y_copies[n, k, d] = send(place, 12, y_recv.at[n, k, d - 1], seg=y_seg(d))
-        send(place, 15, c_recv.at[0], seg=mate)
-
-    def gather_z(n):
-        for k in range(1, half):
-            z_copies[n, k] = send(
-                block(n, 0, ep), 10, ag_recv.at[n, k - 1], ep=lax.rem(ep + 2 * k, ep_count)
-            )
-        spread(n, 0)
-
-    def gather_xy(n):
-        for k in range(1, half):
-            spread(n, k)
-
-    def relay(n):
-        for k in range(half):
-            x_copies[n, k].wait_recv()
-            place = block(n, 0, on_line(x_mate, k))
-            if k not in by_x:
-                for d in range(1, y_count):
-                    send(place, 13, xy_recv.at[n, 0], seg=y_seg(d))
-            send(place, 15, c_recv.at[0], seg=mate)
-            for d in range(1, y_count):
-                y_copies[n, k, d].wait_recv()
-                place = block(n, d, on_line(ep, k))
-                if k in by_x:
-                    send(place, 14, xy_recv.at[n, 1], ep=x_mate)
-                send(place, 15, c_recv.at[d], seg=mate)
+            y_copies[n, k, d].wait_recv()
+            place = block(n, d, on_line(ep, k))
+            if k in by_x:
+                send(place, 14, xy_recv.at[n, 1], ep=x_mate)
+            send(place, 15, c_recv.at[d], seg=mate)
 
     by_y = [k for k in range(half) if k not in by_x]
 
     def blocks(count):
         return full.at[0, 0, pl.ds(0, count)]
 
-    def hand_over(n):
+    def hand_over(end, n):
         for i, ks in enumerate((by_y, by_x)):
             if ks and y_count > 1:
                 collect(blocks(len(ks) * (y_count - 1)), xy_recv.at[n, i])
@@ -550,7 +579,6 @@
                 for d in range(1, y_count):
                     send(block(n, d, on_line(x_mate, k)), 15, c_recv.at[d], seg=mate)
 
-    later(full.at[0, :, pl.ds(0, half - 1)], 10)
     later(full.at[0, :, pl.ds(0, half)], 11)
     if y_count > 1:
         later(full.at[0, :, pl.ds(0, half * (y_count - 1))], 12)
@@ -559,35 +587,41 @@
                 later(full.at[0, :, pl.ds(0, len(ks) * (y_count - 1))], 13 + i)
     later(full.at[pl.ds(0, y_count)], 15)
 
-    def attend():
+    def attend(end):
         mix_all()
 
-    for stage, n in (
-        (project, 1), (combine, 0), (project, 2), (project, 3), (combine, 1), (attend, None),
-        (combine, 2), (finish, 0), (gather_z, 0), (combine, 3), (finish, 1), (gather_z, 1),
-        (gather_xy, 0), (finish, 2), (gather_z, 2), (gather_xy, 1), (relay, 0),
-        (finish, 3), (gather_z, 3), (gather_xy, 2), (relay, 1), (gather_xy, 3), (hand_over, 0),
-        (relay, 2), (hand_over, 1), (relay, 3),
-    ):
-        stage(*([] if n is None else [n]))
+    def proceed(end, start, beat, near_lag, far_lag, first, relay_beat, relay_step, hand_lag, at):
+        plan = [(2.0 * n, project, (n,)) for n in range(1, seg_count)] + [(at, attend, ())]
+        for n in range(seg_count):
+            for p in range(len(pieces)):
+                time = start + beat * (n * len(pieces) + p)
+                plan += [
+                    (time, combine, (n, p)), (time + near_lag, near, (n, p)),
+                    (time + far_lag, far, (n, p)),
+                ]
+            plan += [(time + far_lag + 0.01, spread, (n,))]
+            ready = start + beat * (len(pieces) - 1) + far_lag + first + relay_beat * n
+            plan += [(ready + relay_step * k, relay, (n, k)) for k in range(half)]
+            plan += [(ready + hand_lag, hand_over, (n,))]
+        for _, stage, given in sorted(plan, key=lambda item: item[0]):
+            stage(end, *given)
+
+    for end, hints in zip((True, False), pace):
+        pl.when(at_end if end else jnp.logical_not(at_end))(
+            functools.partial(proceed, end, *hints)
+        )
     loads[1].wait()
     acc[...] = jnp.zeros_like(acc)
 
     def multiply(s):
-        def step(n, carry):
-            at = pl.multiple_of(n * tile, tile)
-            block = full[s, :, :, :, pl.ds(at, tile)].reshape(total, tile)
-            lines = pl.ds(pl.multiple_of(s * cols + n * tile, tile), tile)
-            acc[...] += lax.dot_general(
-                block, up[:, lines], (((1,), (1,)), ((), ())), preferred_element_type=f32
-            )
-            return carry
-
-        lax.fori_loop(0, cols // tile, step, 0)
+        lines = pl.ds(pl.multiple_of(s * cols, cols), cols)
+        acc[...] += lax.dot_general(
+            full[s].reshape(total, cols), up[:, lines], (((1,), (1,)), ((), ())),
+            preferred_element_type=f32,
+        )
 
     multiply(seg)
-    for n in range(2, seg_count):
-        hand_over(n)
+    pass
     for d in range(1, y_count):
         multiply(y_seg(-d))
     tokens[ep] = mix_ref[ep]
@@ -720,6 +754,11 @@
     whole.start()
     for copy in pending:
         copy.wait_send()
+
+    @pl.when(jnp.logical_not(at_end))
+    def _():
+        remote(x_sum, x_sum, one_send.at[10], one_recv.at[0], ep=x_mate).wait_send()
+
     result.wait()
     whole.wait()
 
@@ -763,7 +802,7 @@
     steps = model // wide
     hbm = pl.BlockSpec(memory_space=pl.ANY)
     results = pl.pallas_call(
-        functools.partial(step_kernel, seg_count, ep_count, heads, dim, tile, wide, (1, 6, 11), tuple(range(1, half, 2))),
+        functools.partial(step_kernel, seg_count, ep_count, heads, dim, tile, wide, (1, 6, 11), BYX, PACE),
         out_shape=(
             jax.ShapeDtypeStruct((tokens_own, features), bf16),
             jax.ShapeDtypeStruct((moe_own, model), bf16),
@@ -793,7 +832,10 @@
             VM((seg_count, 2, half, moe_own, cols + 128), bf16),
             VM((seg_count, half, moe_own, cols + 128), bf16),
             VM((seg_count, half, moe_own, cols + 128), bf16),
+            VM((2, seg_count, half, moe_own, cols + 128), bf16),
             VM((seg_count, half, moe_own, cols + 128), bf16),
+            VM((seg_count, half, moe_own, cols + 128), bf16),
+            VM((seg_count, half, moe_own, 128), f32),
             VM((seg_count, seg_count, ep_count, moe_own, cols), bf16),
             VM((total, units), f32),
             VM((total, units), bf16),
@@ -810,9 +852,8 @@
             dma((23,)),
             dma((17,)),
             dma((seg_count - 1,)),
-            dma((seg_count - 1 + cols // tile,)),
-            dma((seg_count,)),
-            dma((seg_count, half - 1)),
+            dma((seg_count, cols // tile)),
+            dma((2, seg_count, cols // tile)),
             dma((seg_count, half)),
             dma((seg_count, half, max(1, y_count - 1))),
             dma((seg_count, 2)),

time: 88.8 us -> 85.7 us (0.965)
  Pallas kernels: 88 us -> 84.8 us
    pallas_call x1, Pallas kernels: 86.3 us -> 83.1 us  [on_device_dense(): pl.pallas_call(functools.partial(step_kernel, seg_count, ep_count, heads,...]
where the time goes in v3:
time: 85.7 us; the launch traced here: 85.6 us
  Pallas kernels  84.8 us (99%)
    pallas_call x1, Pallas kernels, on_device_dense(): pl.pallas_call(functools.partial(step_kernel, seg_count, ep_count, heads,...  83.1 us

profile of v3, /device:TPU:0, one launch (start us, length us, event | category | flops | bytes accessed | tf_op | source)
XLA Modules:
  0.0 85.6 jit_solution(9875519013598227380)
XLA Ops:
  0.6 83.1 %shard_map.113 = (bf16[64,2048]{1,0:T(8,128)(2,1)}, bf16[8,6144]{1,0:T(8,128)(2,1)}) custom-call(bf16[64,2048]{1,0:T(8,128)(2,1)} %q_ref.1, bf16[64,2048]{1,0:T(8,128)(2,1)} %k_ref.1, bf16[64,2048]{1,0:T(8,128)(2,1)} %v_ref.1, bf16[256,1536]{1,0:T(8,128)(2,1)} %proj_hbm.1, bf16[1,576,6144]{2,1,0:T(8,128)(2,1)} %bitcast.5, bf16[1,576,6144]{2,1,0:T(8,128)(2,1)} %down_hbm.1, ...), custom_call_target="tpu_custom_call" | custom-call | tf_op jit(solution)/shard_map/pallas_call | solution.py:804
  83.7 1.7 %shard_map.114 = (bf16[64,2048]{1,0:T(8,128)(2,1)}, bf16[8,6144]{1,0:T(8,128)(2,1)}) custom-call(bf16[64,2048]{1,0:T(8,128)(2,1)} %get-tuple-element.4.a_in, bf16[8,6144]{1,0:T(8,128)(2,1)} %get-tuple-element.5.b_in), custom_call_target="tpu_custom_call" | custom-call | tf_op jit(solution)/shard_map/pallas_call | solution.py:870

commit v4 on v3

--- a/solution.py
+++ b/solution.py
@@ -602,7 +602,8 @@
             plan += [(time + far_lag + 0.01, spread, (n,))]
             ready = start + beat * (len(pieces) - 1) + far_lag + first + relay_beat * n
             plan += [(ready + relay_step * k, relay, (n, k)) for k in range(half)]
-            plan += [(ready + hand_lag, hand_over, (n,))]
+            if n < seg_count - 1:
+                plan += [(ready + hand_lag, hand_over, (n,))]
         for _, stage, given in sorted(plan, key=lambda item: item[0]):
             stage(end, *given)
 
@@ -611,19 +612,23 @@
             functools.partial(proceed, end, *hints)
         )
     loads[1].wait()
-    acc[...] = jnp.zeros_like(acc)
-
-    def multiply(s):
+
+    def multiply(s, fresh=False):
         lines = pl.ds(pl.multiple_of(s * cols, cols), cols)
-        acc[...] += lax.dot_general(
+        value = lax.dot_general(
             full[s].reshape(total, cols), up[:, lines], (((1,), (1,)), ((), ())),
             preferred_element_type=f32,
         )
-
-    multiply(seg)
-    pass
-    for d in range(1, y_count):
-        multiply(y_seg(-d))
+        acc[...] = value if fresh else acc[...] + value
+
+    multiply(seg, True)
+    for k in range(y_count):
+        waiter(full.at[0], c_recv.at[k], seg=mate).wait_recv()
+        multiply(seg_at(-k, 1))
+        if k == 0:
+            hand_over(None, seg_count - 1)
+        if k + 1 < y_count:
+            multiply(y_seg(-k - 1))
     tokens[ep] = mix_ref[ep]
     for j in range(1, ep_count):
         other = lax.rem(ep + j, ep_count)
@@ -631,9 +636,6 @@
             mix_ref.at[other], tokens.at[ep], one_send.at[16], one_recv.at[16], ep=other
         ).start()
     later(tokens.at[others], 16)
-    for k in range(y_count):
-        waiter(full.at[0], c_recv.at[k], seg=mate).wait_recv()
-        multiply(seg_at(-k, 1))
     value = acc[...]
     hidden[...] = (value / (1.0 + jnp.exp(-value))).astype(bf16)
     collect(table_ref.at[other_segs], one_recv.at[9])
@@ -802,7 +804,7 @@
     steps = model // wide
     hbm = pl.BlockSpec(memory_space=pl.ANY)
     results = pl.pallas_call(
-        functools.partial(step_kernel, seg_count, ep_count, heads, dim, tile, wide, (1, 6, 11), BYX, PACE),
+        functools.partial(step_kernel, seg_count, ep_count, heads, dim, tile, wide, (2, 8, 13), BYX, PACE),
         out_shape=(
             jax.ShapeDtypeStruct((tokens_own, features), bf16),
             jax.ShapeDtypeStruct((moe_own, model), bf16),

time: 85.7 us -> 84.8 us (0.989)
  Pallas kernels: 84.8 us -> 83.8 us
    pallas_call x1, Pallas kernels: 83.1 us -> 82.1 us  [on_device_dense(): pl.pallas_call(functools.partial(step_kernel, seg_count, ep_count, heads,...]
where the time goes in v4:
time: 84.8 us; the launch traced here: 84.6 us
  Pallas kernels  83.8 us (99%)
    pallas_call x1, Pallas kernels, on_device_dense(): pl.pallas_call(functools.partial(step_kernel, seg_count, ep_count, heads,...  82.1 us
    pallas_call x1, Pallas kernels, on_device_dense(): pl.pallas_call(carry_kernel, out_shape=tuple((jax.ShapeDtypeStruct(r.shap...  1.71 us

profile of v4, /device:TPU:0, one launch (start us, length us, event | category | flops | bytes accessed | tf_op | source)
XLA Modules:
  0.0 84.6 jit_solution(10769127021232715655)
XLA Ops:
  0.6 82.1 %shard_map.113 = (bf16[64,2048]{1,0:T(8,128)(2,1)}, bf16[8,6144]{1,0:T(8,128)(2,1)}) custom-call(bf16[64,2048]{1,0:T(8,128)(2,1)} %q_ref.1, bf16[64,2048]{1,0:T(8,128)(2,1)} %k_ref.1, bf16[64,2048]{1,0:T(8,128)(2,1)} %v_ref.1, bf16[256,1536]{1,0:T(8,128)(2,1)} %proj_hbm.1, bf16[1,576,6144]{2,1,0:T(8,128)(2,1)} %bitcast.5, bf16[1,576,6144]{2,1,0:T(8,128)(2,1)} %down_hbm.1, ...), custom_call_target="tpu_custom_call" | custom-call | tf_op jit(solution)/shard_map/pallas_call | solution.py:806
  82.7 1.7 %shard_map.114 = (bf16[64,2048]{1,0:T(8,128)(2,1)}, bf16[8,6144]{1,0:T(8,128)(2,1)}) custom-call(bf16[64,2048]{1,0:T(8,128)(2,1)} %get-tuple-element.4.a_in, bf16[8,6144]{1,0:T(8,128)(2,1)} %get-tuple-element.5.b_in), custom_call_target="tpu_custom_call" | custom-call | tf_op jit(solution)/shard_map/pallas_call | solution.py:872

commit v5 on v4

--- a/solution.py
+++ b/solution.py
@@ -244,7 +244,7 @@
         pending.append(remote(ref, ref, one_send.at[index], one_recv.at[0], ep=x_mate))
 
     def scatter(ref, buf, index):
-        for j in range(1, ep_count):
+        for j in sorted(range(1, ep_count), key=lambda j: abs(2 * j - ep_count)):
             other = lax.rem(ep + j, ep_count)
             columns = pl.ds(pl.multiple_of(other * width, width), width)
             remote(

time: 84.8 us -> 84.3 us (level)
  no operation moved by 1% of the time
where the time goes in v5:
time: 84.3 us; the launch traced here: 84.1 us
  Pallas kernels  83.3 us (99%)
    pallas_call x1, Pallas kernels, on_device_dense(): pl.pallas_call(functools.partial(step_kernel, seg_count, ep_count, heads,...  81.6 us
    pallas_call x1, Pallas kernels, on_device_dense(): pl.pallas_call(carry_kernel, out_shape=tuple((jax.ShapeDtypeStruct(r.shap...  1.71 us

profile of v5, /device:TPU:0, one launch (start us, length us, event | category | flops | bytes accessed | tf_op | source)
XLA Modules:
  0.0 84.1 jit_solution(293951248615042036)
XLA Ops:
  0.6 81.6 %shard_map.113 = (bf16[64,2048]{1,0:T(8,128)(2,1)}, bf16[8,6144]{1,0:T(8,128)(2,1)}) custom-call(bf16[64,2048]{1,0:T(8,128)(2,1)} %q_ref.1, bf16[64,2048]{1,0:T(8,128)(2,1)} %k_ref.1, bf16[64,2048]{1,0:T(8,128)(2,1)} %v_ref.1, bf16[256,1536]{1,0:T(8,128)(2,1)} %proj_hbm.1, bf16[1,576,6144]{2,1,0:T(8,128)(2,1)} %bitcast.5, bf16[1,576,6144]{2,1,0:T(8,128)(2,1)} %down_hbm.1, ...), custom_call_target="tpu_custom_call" | custom-call | tf_op jit(solution)/shard_map/pallas_call | solution.py:806
  82.3 1.7 %shard_map.114 = (bf16[64,2048]{1,0:T(8,128)(2,1)}, bf16[8,6144]{1,0:T(8,128)(2,1)}) custom-call(bf16[64,2048]{1,0:T(8,128)(2,1)} %get-tuple-element.4.a_in, bf16[8,6144]{1,0:T(8,128)(2,1)} %get-tuple-element.5.b_in), custom_call_target="tpu_custom_call" | custom-call | tf_op jit(solution)/shard_map/pallas_call | solution.py:872

commit v6 on v5

--- a/solution.py
+++ b/solution.py
@@ -275,7 +275,7 @@
     ).astype(bf16)
     for p in range(ep_count):
         q_out[p] = chosen[:, p * width : (p + 1) * width]
-    for j in range(1, ep_count):
+    for j in sorted(range(1, ep_count), key=lambda j: abs(2 * j - ep_count)):
         other = lax.rem(ep + j, ep_count)
         remote(q_out.at[other], q_in.at[ep], one_send.at[2], one_recv.at[2], ep=other).start()
     later(q_in.at[others], 2)
@@ -630,7 +630,7 @@
         if k + 1 < y_count:
             multiply(y_seg(-k - 1))
     tokens[ep] = mix_ref[ep]
-    for j in range(1, ep_count):
+    for j in sorted(range(1, ep_count), key=lambda j: abs(2 * j - ep_count)):
         other = lax.rem(ep + j, ep_count)
         remote(
             mix_ref.at[other], tokens.at[ep], one_send.at[16], one_recv.at[16], ep=other

time: 84.3 us -> 84.5 us (level)
  no operation moved by 1% of the time
where the time goes in v6:
time: 84.5 us; the launch traced here: 84.3 us
  Pallas kernels  83.5 us (99%)
    pallas_call x1, Pallas kernels, on_device_dense(): pl.pallas_call(functools.partial(step_kernel, seg_count, ep_count, heads,...  81.8 us
    pallas_call x1, Pallas kernels, on_device_dense(): pl.pallas_call(carry_kernel, out_shape=tuple((jax.ShapeDtypeStruct(r.shap...  1.71 us

profile of v6, /device:TPU:0, one launch (start us, length us, event | category | flops | bytes accessed | tf_op | source)
XLA Modules:
  0.0 84.3 jit_solution(2854436697443255284)
XLA Ops:
  0.6 81.8 %shard_map.113 = (bf16[64,2048]{1,0:T(8,128)(2,1)}, bf16[8,6144]{1,0:T(8,128)(2,1)}) custom-call(bf16[64,2048]{1,0:T(8,128)(2,1)} %q_ref.1, bf16[64,2048]{1,0:T(8,128)(2,1)} %k_ref.1, bf16[64,2048]{1,0:T(8,128)(2,1)} %v_ref.1, bf16[256,1536]{1,0:T(8,128)(2,1)} %proj_hbm.1, bf16[1,576,6144]{2,1,0:T(8,128)(2,1)} %bitcast.5, bf16[1,576,6144]{2,1,0:T(8,128)(2,1)} %down_hbm.1, ...), custom_call_target="tpu_custom_call" | custom-call | tf_op jit(solution)/shard_map/pallas_call | solution.py:806
  82.4 1.7 %shard_map.114 = (bf16[64,2048]{1,0:T(8,128)(2,1)}, bf16[8,6144]{1,0:T(8,128)(2,1)}) custom-call(bf16[64,2048]{1,0:T(8,128)(2,1)} %get-tuple-element.4.a_in, bf16[8,6144]{1,0:T(8,128)(2,1)} %get-tuple-element.5.b_in), custom_call_target="tpu_custom_call" | custom-call | tf_op jit(solution)/shard_map/pallas_call | solution.py:872
